TPU v7x, 128 devices: a whole 4x4x4 slice. The times are simulated.
128 devices in a mesh: vec: 16 (over y, x_lo, core), cent: 8 (over x_hi, z).
Axes of the slice: x: 4 (x_hi: 2, x_lo: 2; x = x_hi * 2 + x_lo), y: 4, z: 4, core: 2. Of those that a mesh axis runs over, the one named last changes fastest.
Arguments:
- weights: bfloat16 [32768, 256], P('vec'), may hold values from -44 to 44
- centroids: bfloat16 [8192, 256], P('cent'), may hold values from -4 to 4
- cotangent: bfloat16 [32768, 256], P('vec'), may hold values from -6 to 6
Outputs:
- grad_weights: bfloat16 [32768, 256], P('vec')
- grad_centroids: float32 [8192, 256], P('cent')
All inputs are finite; a program needn't handle non-finite values.
Results may differ from a plain program's by a relative error of at most 0.02.
The roundings to bfloat16 on the way count: a program that leaves them out, or rounds other values in their place, can miss the bound.
Values may be sent and summed in bfloat16 or wider, within the bound.
A program may use at most 128 MiB of HBM per device.

v0:
```python
import jax
import jax.numpy as jnp
from jax import lax
from jax.sharding import PartitionSpec as P

D = 256


def from_everyone(value, axis):
    peers = lax.axis_size(axis)
    return lax.all_to_all(
        jnp.broadcast_to(value[None], (peers, *value.shape)), axis, 0, 0, tiled=True
    )


def gathered_once(value, axis):
    leaves = jax.tree.leaves(value)
    turns = sorted(range(len(leaves)), key=lambda k: -leaves[k].size)
    width = (1, *leaves[turns[0]].shape)[-1]
    lines = [
        jnp.pad(leaves[k].reshape(-1), (0, -leaves[k].size % width)).reshape(-1, width)
        for k in turns
    ]
    both, at, found = (from_everyone(jnp.concatenate(lines), axis), 0, {})
    for k, line in zip(turns, lines):
        share = both[:, at : at + len(line)].reshape(len(both), -1)
        found[k] = share[:, : leaves[k].size].reshape(-1, *leaves[k].shape)
        at += len(line)
    numbers = iter(range(len(leaves)))
    return jax.tree.map(lambda _: found[next(numbers)], value)


def joined_by_halves(pieces, combine):
    while len(jax.tree.leaves(pieces)[0]) > 1:
        pieces = jax.vmap(combine)(
            *(jax.tree.map(lambda part: part[side::2], pieces) for side in (0, 1))
        )
    return jax.tree.map(lambda part: part[0], pieces)


def merged(value, axis, combine):
    pieces = gathered_once(value, axis)
    return joined_by_halves(pieces, combine)


def over_copies(value, axis):
    everything = from_everyone(value, axis)
    return jnp.sum(everything, axis=0)


def laid_out(tiles, dim):
    dims = list(tiles.shape[1:])
    dims[dim] *= tiles.shape[0]
    return jnp.moveaxis(tiles, 0, dim).reshape(dims)


def gather_directly(value, axis, dim):
    return laid_out(from_everyone(value, axis), dim)


def in_blocks(value, dim, peers):
    before, after = (value.shape[:dim], value.shape[dim + 1 :])
    return jnp.moveaxis(value.reshape(*before, peers, -1, *after), dim, 0)


def sent_and_summed(value, axis, dim):
    peers = lax.axis_size(axis)
    tiles = lax.all_to_all(in_blocks(value, dim, peers), axis, 0, 0, tiled=True)
    return jnp.sum(tiles.astype(jnp.float32), axis=0)


def filled_up(lines, peers):
    spare = -lines.shape[0] % peers
    if not spare:
        return lines
    return jnp.concatenate([lines, jnp.zeros((spare, *lines.shape[1:]), lines.dtype)])


def total_of(value, axis):
    lines = value.reshape(-1, *value.shape[1:][-1:])
    own = lax.psum_scatter(
        filled_up(lines, lax.axis_size(axis)), axis, scatter_dimension=0, tiled=True
    )
    whole = lax.all_gather(own, axis).reshape(-1, *lines.shape[1:])
    return lax.slice_in_dim(whole, 0, len(lines)).reshape(value.shape)


def sent_and_summed_2(value, axis, dim):
    peers = lax.axis_size(axis)
    tiles = lax.all_to_all(in_blocks(value, dim, peers), axis, 0, 0, tiled=True)
    return jnp.sum(tiles, axis=0)


def logits(rows, cent):
    cross = jnp.dot(rows, cent.T, preferred_element_type=jnp.float32)
    square = jnp.sum(jnp.square(cent.astype(jnp.float32)), axis=1)
    return (2.0 * cross - square[None, :]) * D ** (-0.5)


def combine_stats(first, second):
    peak = jnp.maximum(first[0], second[0])
    total = first[1] * jnp.exp(first[0] - peak) + second[1] * jnp.exp(second[0] - peak)
    return (peak, total)


def soften(score):
    top = jnp.max(score, axis=1)
    local = jnp.sum(jnp.exp(score - top[:, None]), axis=1)
    peak, total = merged((top, local), "cent", combine_stats)
    expo = jnp.exp(score - peak[:, None])
    return expo / total[:, None]


def row_dot(resp, dresp):
    return over_copies(jnp.sum(resp * dresp, axis=1), "cent")


def body(weights, centroids, cotangent):
    scale = 2.0 * D ** (-0.5)
    resp = soften(logits(weights, centroids))
    resp_b = resp.astype(jnp.bfloat16)
    mass = jnp.dot(resp_b.T, weights, preferred_element_type=jnp.float32)
    count = jnp.sum(resp, axis=0)
    mass, count = (
        lax.psum_scatter(mass, "vec", scatter_dimension=0, tiled=True),
        lax.psum_scatter(count, "vec", scatter_dimension=0, tiled=True),
    )
    denom = count + 1e-06
    moved = gather_directly((mass / denom[:, None]).astype(jnp.bfloat16), "vec", 0)
    moved_f = moved.astype(jnp.float32)
    resp_two = soften(logits(weights, moved))
    dresp_two = jnp.dot(cotangent, moved.T, preferred_element_type=jnp.float32)
    dots_two = row_dot(resp_two, dresp_two)
    edge_two = resp_two * (dresp_two - dots_two[:, None]) * scale
    edge_two_b = edge_two.astype(jnp.bfloat16)
    part_two = jnp.dot(edge_two_b, moved, preferred_element_type=jnp.float32)
    moved_cot = jnp.dot(
        resp_two.astype(jnp.bfloat16).T, cotangent, preferred_element_type=jnp.float32
    )
    moved_cot = moved_cot + jnp.dot(edge_two_b.T, weights, preferred_element_type=jnp.float32)
    moved_cot = moved_cot - jnp.sum(edge_two, axis=0)[:, None] * moved_f
    moved_cot = sent_and_summed(moved_cot.astype(jnp.bfloat16), "vec", 0)
    mean_cot = gather_directly((moved_cot / denom[:, None]).astype(jnp.bfloat16), "vec", 0)
    count_cot = -jnp.sum(mean_cot.astype(jnp.float32) * moved_f, axis=1)
    dresp_one = (
        jnp.dot(weights, mean_cot.T, preferred_element_type=jnp.float32) + count_cot[None, :]
    )
    dots_one = row_dot(resp, dresp_one)
    edge_one = resp * (dresp_one - dots_one[:, None]) * scale
    edge_one_b = edge_one.astype(jnp.bfloat16)
    total = part_two + jnp.dot(resp_b, mean_cot, preferred_element_type=jnp.float32)
    total = total + jnp.dot(edge_one_b, centroids, preferred_element_type=jnp.float32)
    start_cot = jnp.dot(edge_one_b.T, weights, preferred_element_type=jnp.float32)
    start_cot = start_cot - jnp.sum(edge_one, axis=0)[:, None] * centroids.astype(jnp.float32)
    start_cot = total_of(start_cot.astype(jnp.bfloat16), "vec").astype(jnp.float32)
    share = sent_and_summed_2(total, "cent", 0).astype(jnp.bfloat16)
    grad_rows = gather_directly(share, "cent", 0)
    return (grad_rows, start_cot)


def solution(mesh):
    return jax.shard_map(
        body,
        mesh=mesh,
        in_specs=(P("vec", None), P("cent", None), P("vec", None)),
        out_specs=(P("vec", None), P("cent", None)),
        check_vma=False,
    )
```

profile of v0, /device:TPU:0, one launch (start us, length us, event | category | flops | bytes accessed | tf_op | source)
XLA Modules:
  0.0 331.6 jit_solution(2056726963172004796)
XLA Ops:
  16.7 15.8 %all_to_all.47 = f32[8,2,2048]{2,1,0:T(2,128)S(1)} all-to-all(f32[8,2,2048]{2,1,0:T(2,128)S(1)} %broadcast_in_dim.14), channel_id=1, replica_groups=mesh['vec'=16,'cent'=8] {'cent'}, dimensions={0} | all-to-all | bytes 262144 | tf_op jit(solution)/shard_map/all_to_all | solution.py:11
  33.0 4.8 %fusion.33 = (f32[1024]{0:T(1024)S(1)}, f32[2048,1024]{0,1:T(8,128)S(1)}) fusion(f32[2048]{0:T(1024)S(1)} %bitcast.100, f32[2048]{0:T(1024)S(1)} %bitcast.101, f32[1024]{0:T(1024)S(1)} %fusion.26, f32[2048,1024]{0,1:T(8,128)} %copy-done.3), kind=kLoop, calls=%fused_computation.65 | loop fusion | flops 12581888 | bytes 16801792 | tf_op jit(solution)/shard_map/reduce_sum | solution.py:123
  44.6 28.2 %all-reduce = f32[1024]{0:T(1024)S(1)} all-reduce(f32[1024]{0:T(1024)S(1)} %get-tuple-element.10), channel_id=4, replica_groups=mesh['vec'=16,'cent'=8] {'vec'}, use_global_device_ids=true, to_apply=%region_5.6.clone | all-reduce | flops 1024 | bytes 8192
  72.8 30.3 %reduce-scatter.3.cloned.1.call-done = f32[64,256]{1,0:T(8,128)} async-done(((f32[1024,256]{1,0:T(8,128)}), f32[64,256]{1,0:T(8,128)}) %reduce-scatter.3.cloned.1.call-update) | async-done | bytes 65552 | tf_op jit(solution)/shard_map/reduce_scatter | solution.py:125
  104.1 13.5 %all_to_all.48 = bf16[16,64,256]{2,1,0:T(8,128)(2,1)S(1)} all-to-all(bf16[16,64,256]{2,1,0:T(8,128)(2,1)S(1)} %broadcast_in_dim.15), channel_id=1, replica_groups=mesh['vec'=16,'cent'=8] {'vec'}, dimensions={0} | all-to-all | bytes 1048576 | tf_op jit(solution)/shard_map/all_to_all | solution.py:11
  125.2 14.7 %all_to_all.49 = f32[8,2,2048]{2,1,0:T(2,128)S(1)} all-to-all(f32[8,2,2048]{2,1,0:T(2,128)S(1)} %broadcast_in_dim.16), channel_id=1, replica_groups=mesh['vec'=16,'cent'=8] {'cent'}, dimensions={0} | all-to-all | bytes 262144 | tf_op jit(solution)/shard_map/all_to_all | solution.py:11
  140.5 7.1 %fusion.3 = (f32[2048]{0:T(1024)S(1)}, f32[1024,2048]{1,0:T(8,128)}) fusion(f32[2048]{0:T(1024)S(1)} %bitcast.94, f32[2048]{0:T(1024)S(1)} %bitcast.97, f32[1024]{0:T(1024)S(1)} %sub.132, f32[1024,2048]{1,0:T(8,128)} %copy-done.2, bf16[1024,256]{1,0:T(8,128)(2,1)S(1)} %bitcast.84, bf16[2048,256]{1,0:T(8,128)(2,1)S(1)} %copy-done.8), kind=kOutput, calls=%fused_computation.7 | convolution fusion | flops 1088419840 | bytes 18378752 | tf_op jit(solution)/shard_map/dot_general | solution.py:132
  147.6 10.4 %all_to_all.50 = f32[8,1,2048]{2,1,0:T(1,128)S(1)} all-to-all(f32[8,1,2048]{2,1,0:T(1,128)S(1)} %broadcast_in_dim.17), channel_id=1, replica_groups=mesh['vec'=16,'cent'=8] {'cent'}, dimensions={0} | all-to-all | bytes 131072 | tf_op jit(solution)/shard_map/all_to_all | solution.py:11
  158.0 7.7 %fusion.9 = (f32[1024]{0:T(1024)S(1)}, bf16[2048,1024]{0,1:T(8,128)(2,1)S(1)}) fusion(f32[2048]{0:T(1024)S(1)} %reduce_sum.132, f32[1024,2048]{1,0:T(8,128)} %get-tuple-element.29, f32[2048]{0:T(1024)S(1)} %bitcast.95, f32[2048]{0:T(1024)S(1)} %bitcast.98, f32[1024]{0:T(1024)S(1)} %sub.132, f32[1024,2048]{1,0:T(8,128)} %copy-done.2), kind=kLoop, calls=%fused_computation.20 | loop fusion | flops 20970496 | bytes 21004288 | tf_op jit(solution)/shard_map/reduce_sum | solution.py:141
  167.0 5.9 %fusion.22 = bf16[1024,256]{1,0:T(8,128)(2,1)S(1)} fusion(f32[1024,256]{1,0:T(8,128)S(1)} %fusion.37, bf16[2048,256]{1,0:T(8,128)(2,1)S(1)} %copy-done.8, bf16[1024,256]{1,0:T(8,128)(2,1)S(1)} %bitcast.85, f32[1024]{0:T(1024)S(1)} %get-tuple-element.18, f32[1024,2048]{1,0:T(8,128)} %copy-done.2, f32[2048]{0:T(1024)S(1)} %bitcast.96, f32[2048]{0:T(1024)S(1)} %bitcast.99, ...), kind=kOutput, calls=%fused_computation.37 | convolution fusion | flops 1087635456 | bytes 11558912 | tf_op jit(solution)/shard_map/dot_general | solution.py:137
  172.9 13.5 %all_to_all.51 = bf16[16,64,256]{2,1,0:T(8,128)(2,1)S(1)} all-to-all(bf16[16,64,256]{2,1,0:T(8,128)(2,1)S(1)} %bitcast.89), channel_id=1, replica_groups=mesh['vec'=16,'cent'=8] {'vec'}, dimensions={0} | all-to-all | bytes 1048576 | tf_op jit(solution)/shard_map/all_to_all | solution.py:68
  187.3 3.6 %all-to-all-start.5 = ((bf16[16,64,256]{2,1,0:T(8,128)(2,1)}), bf16[16,64,256]{2,1,0:T(8,128)(2,1)S(1)}, u32[]{:S(2)}, u32[]{:S(2)}) async-start(bf16[16,64,256]{2,1,0:T(8,128)(2,1)} %broadcast_in_dim.18), calls=%async_computation.6 | async-start | bytes 1048576 | tf_op jit(solution)/shard_map/all_to_all | solution.py:11
  190.9 4.8 %fusion.36 = f32[2048,256]{1,0:T(8,128)} fusion(bf16[2048,1024]{0,1:T(8,128)(2,1)} %copy-done.5, bf16[1024,256]{1,0:T(8,128)(2,1)S(1)} %bitcast.86), kind=kOutput, calls=%fused_computation.68 | convolution fusion | flops 1073741824 | bytes 6815744 | tf_op jit(solution)/shard_map/dot_general | solution.py:136
  195.7 6.0 %all-to-all-done.5 = bf16[16,64,256]{2,1,0:T(8,128)(2,1)S(1)} async-done(((bf16[16,64,256]{2,1,0:T(8,128)(2,1)}), bf16[16,64,256]{2,1,0:T(8,128)(2,1)S(1)}, u32[]{:S(2)}, u32[]{:S(2)}) %all-to-all-start.5) | async-done | bytes 524320 | tf_op jit(solution)/shard_map/all_to_all | solution.py:11
  202.0 7.9 %fusion = (f32[2048]{0:T(1024)S(1)}, f32[1024,2048]{1,0:T(8,128)}) fusion(f32[2048,1024]{0,1:T(8,128)} %copy-done.1, f32[1024]{0:T(1024)S(1)} %neg.11, bf16[1024,256]{1,0:T(8,128)(2,1)S(1)} %bitcast.81, bf16[2048,256]{1,0:T(8,128)(2,1)S(1)} %copy-done), kind=kOutput, calls=%fused_computation.2 | convolution fusion | flops 1080031232 | bytes 18362368 | tf_op jit(solution)/shard_map/dot_general | solution.py:146
  210.5 3.6 %all-to-all-start.6 = ((f32[8,1,2048]{2,1,0:T(1,128)}), f32[8,1,2048]{2,1,0:T(1,128)S(1)}, u32[]{:S(2)}, u32[]{:S(2)}) async-start(f32[8,1,2048]{2,1,0:T(1,128)} %broadcast_in_dim.19), calls=%async_computation.7 | async-start | bytes 131072 | tf_op jit(solution)/shard_map/all_to_all | solution.py:11
  214.1 6.6 %convolution_add_fusion.1 = f32[2048,256]{1,0:T(8,128)} fusion(f32[2048,256]{1,0:T(8,128)} %fusion.36, bf16[1024,256]{1,0:T(8,128)(2,1)S(1)} %bitcast.82, f32[2048,1024]{0,1:T(8,128)} %copy-done.1), kind=kOutput, calls=%fused_computation.23 | convolution fusion | flops 1076363264 | bytes 13107200 | tf_op jit(solution)/shard_map/dot_general | solution.py:151
  221.8 7.0 %fusion.31 = (f32[1024]{0:T(1024)S(1)}, bf16[2048,1024]{0,1:T(8,128)(2,1)S(1)}) fusion(f32[2048,1024]{0,1:T(8,128)} %copy-done.1, f32[2048]{0:T(1024)S(1)} %reduce_sum.137, f32[1024,2048]{1,0:T(8,128)} %get-tuple-element.31, f32[1024]{0:T(1024)S(1)} %neg.11), kind=kLoop, calls=%fused_computation.64 | loop fusion | flops 12581888 | bytes 20987904 | tf_op jit(solution)/shard_map/reduce_sum | solution.py:154
  231.5 6.0 %all-to-all-start.7 = ((f32[8,256,256]{2,1,0:T(8,128)}), f32[8,256,256]{2,1,0:T(8,128)S(1)}, u32[]{:S(2)}, u32[]{:S(2)}) async-start(f32[8,256,256]{2,1,0:T(8,128)} %bitcast.88), calls=%async_computation.8 | async-start | bytes 4194304 | tf_op jit(solution)/shard_map/all_to_all | solution.py:90
  237.6 4.3 %fusion.23 = bf16[1024,256]{1,0:T(8,128)(2,1)} fusion(bf16[2048,256]{1,0:T(8,128)(2,1)S(1)} %copy-done, bf16[2048,1024]{0,1:T(8,128)(2,1)} %copy-done.6, bf16[1024,256]{1,0:T(8,128)(2,1)} %param.4, f32[1024]{0:T(1024)S(1)} %get-tuple-element.2), kind=kOutput, calls=%fused_computation.38 | convolution fusion | flops 1074790400 | bytes 6295552 | tf_op jit(solution)/shard_map/dot_general | solution.py:153
  241.9 22.3 %all-to-all-done.7 = f32[8,256,256]{2,1,0:T(8,128)S(1)} async-done(((f32[8,256,256]{2,1,0:T(8,128)}), f32[8,256,256]{2,1,0:T(8,128)S(1)}, u32[]{:S(2)}, u32[]{:S(2)}) %all-to-all-start.7) | async-done | bytes 2097184 | tf_op jit(solution)/shard_map/all_to_all | solution.py:90
  265.4 4.2 %all-to-all-start.8 = ((bf16[8,256,256]{2,1,0:T(8,128)(2,1)}), bf16[8,256,256]{2,1,0:T(8,128)(2,1)S(1)}, u32[]{:S(2)}, u32[]{:S(2)}) async-start(bf16[8,256,256]{2,1,0:T(8,128)(2,1)} %broadcast_in_dim.20), calls=%async_computation.9 | async-start | bytes 2097152 | tf_op jit(solution)/shard_map/all_to_all | solution.py:11
  269.7 34.1 %reduce-scatter.5.cloned.1.call-done = bf16[64,256]{1,0:T(8,128)(2,1)} async-done(((bf16[1024,256]{1,0:T(8,128)(2,1)}), bf16[64,256]{1,0:T(8,128)(2,1)}) %reduce-scatter.5.cloned.1.call-update) | async-done | bytes 32784 | tf_op jit(solution)/shard_map/reduce_scatter | solution.py:81
  303.8 19.0 %all-gather = bf16[1024,256]{1,0:T(8,128)(2,1)S(1)} all-gather(bf16[64,256]{1,0:T(8,128)(2,1)} %reduce-scatter.5.cloned.1.call-done), channel_id=2, replica_groups=mesh['vec'=16,'cent'=8] {'vec'}, dimensions={0}, use_global_device_ids=true | all-gather | bytes 557056 | tf_op jit(solution)/shard_map/all_gather | solution.py:84
  (85 shorter events, 35.4 us)
Async XLA Ops:
  7.2 1.4 copy-start
  7.2 96.0 %reduce-scatter.3.cloned.1.call-start = ((), (), s32[]{:S(2)}) async-start(), calls=%async_computation.11 | async-start | bytes 1114112 | tf_op jit(solution)/shard_map/reduce_scatter | solution.py:125
  10.9 3.2 copy-start.3
  37.9 3.2 copy-start.1
  37.9 5.5 %copy-start.9 = (u32[128]{0:T(128)S(1)}, u32[128]{0:T(128)}, u32[]{:S(2)}) copy-start(u32[128]{0:T(128)} %constant.15) | copy-start | bytes 1540
  119.5 3.2 copy-start.2
  119.5 21.0 %copy-start.8 = (bf16[2048,256]{1,0:T(8,128)(2,1)S(1)}, bf16[2048,256]{1,0:T(8,128)(2,1)}, u32[]{:S(2)}) copy-start(bf16[2048,256]{1,0:T(8,128)(2,1)} %param.5) | copy-start | bytes 3145732
  165.7 7.1 %copy-start.5 = (bf16[2048,1024]{0,1:T(8,128)(2,1)}, bf16[2048,1024]{0,1:T(8,128)(2,1)S(1)}, u32[]{:S(2)}) copy-start(bf16[2048,1024]{0,1:T(8,128)(2,1)S(1)} %get-tuple-element.19) | copy-start | bytes 12582916
  187.3 14.4 %all-to-all-start.5 = ((bf16[16,64,256]{2,1,0:T(8,128)(2,1)}), bf16[16,64,256]{2,1,0:T(8,128)(2,1)S(1)}, u32[]{:S(2)}, u32[]{:S(2)}) async-start(bf16[16,64,256]{2,1,0:T(8,128)(2,1)} %broadcast_in_dim.18), calls=%async_computation.6 | async-start | bytes 1048576 | tf_op jit(solution)/shard_map/all_to_all | solution.py:11
  210.5 11.1 %all-to-all-start.6 = ((f32[8,1,2048]{2,1,0:T(1,128)}), f32[8,1,2048]{2,1,0:T(1,128)S(1)}, u32[]{:S(2)}, u32[]{:S(2)}) async-start(f32[8,1,2048]{2,1,0:T(1,128)} %broadcast_in_dim.19), calls=%async_computation.7 | async-start | bytes 131072 | tf_op jit(solution)/shard_map/all_to_all | solution.py:11
  221.7 7.0 %copy-start.4 = (f32[2048,256]{1,0:T(8,128)S(1)}, f32[2048,256]{1,0:T(8,128)}, u32[]{:S(2)}) copy-start(f32[2048,256]{1,0:T(8,128)} %convolution_add_fusion.1) | copy-start | bytes 6291460
  221.8 7.0 %copy-start.7 = (bf16[1024,256]{1,0:T(8,128)(2,1)S(1)}, bf16[1024,256]{1,0:T(8,128)(2,1)}, u32[]{:S(2)}) copy-start(bf16[1024,256]{1,0:T(8,128)(2,1)} %param.4) | copy-start | bytes 1572868
  228.7 2.8 copy-start.6
  231.5 32.7 %all-to-all-start.7 = ((f32[8,256,256]{2,1,0:T(8,128)}), f32[8,256,256]{2,1,0:T(8,128)S(1)}, u32[]{:S(2)}, u32[]{:S(2)}) async-start(f32[8,256,256]{2,1,0:T(8,128)} %bitcast.88), calls=%async_computation.8 | async-start | bytes 4194304 | tf_op jit(solution)/shard_map/all_to_all | solution.py:90
  237.5 66.2 %reduce-scatter.5.cloned.1.call-start = ((), (), s32[]{:S(2)}) async-start(), calls=%async_computation.12 | async-start | bytes 557056 | tf_op jit(solution)/shard_map/reduce_scatter | solution.py:81
  265.4 58.4 %all-to-all-start.8 = ((bf16[8,256,256]{2,1,0:T(8,128)(2,1)}), bf16[8,256,256]{2,1,0:T(8,128)(2,1)S(1)}, u32[]{:S(2)}, u32[]{:S(2)}) async-start(bf16[8,256,256]{2,1,0:T(8,128)(2,1)} %broadcast_in_dim.20), calls=%async_computation.9 | async-start | bytes 2097152 | tf_op jit(solution)/shard_map/all_to_all | solution.py:11
Sparse Core Ops, SparseCore 0:
  43.4 59.6 reduce-scatter.2
  242.1 61.6 reduce-scatter.4
where the time goes:
time: 334 us; the launch traced here: 332 us
  blocking collectives  115 us (34%)
  waiting for transfers between devices  93.6 us (28%)
  matrix products  46.8 us (14%)
  other arithmetic  28.9 us (9%)
  starting transfers between devices  17.5 us (5%)
  between operations  15.1 us (5%)
  local copies, waits for them, and re-layouts  14.8 us (4%)
    all_to_all x4, blocking collectives, from_everyone(): lax.all_to_all(jnp.broadcast_to(value[None], (peers, *value.shape)), axis...  54.3 us
    reduce_scatter x1, waiting for transfers between devices, total_of(): lax.psum_scatter(filled_up(lines, lax.axis_size(axis)), axis, scatter_dim...  34.1 us
    reduce_scatter x1, waiting for transfers between devices, body(): lax.psum_scatter(mass, 'vec', scatter_dimension=0, tiled=True)  30.3 us
    unnamed x1, blocking collectives  28.2 us
    all_to_all x1, waiting for transfers between devices, sent_and_summed_2(): tiles = lax.all_to_all(in_blocks(value, dim, peers), axis, 0, 0, tiled=True)  22.3 us
    all_gather x1, blocking collectives, total_of(): whole = lax.all_gather(own, axis).reshape(-1, *lines.shape[1:])  19 us
    all_to_all x1, blocking collectives, sent_and_summed(): tiles = lax.all_to_all(in_blocks(value, dim, peers), axis, 0, 0, tiled=True)  13.5 us
    all_to_all x3, starting transfers between devices, from_everyone(): lax.all_to_all(jnp.broadcast_to(value[None], (peers, *value.shape)), axis...  11.4 us
  transfers between devices with their start and end apart: 6, of which 5 were waited for; matrix products, arithmetic and copies ran while one was open for 6% of the time, Pallas kernels for 0%

commit v1 on v0

v1 whole, which is shorter than its diff:
```python
import functools
import math

import jax
import jax.numpy as jnp
from jax import lax
from jax.experimental import pallas as pl
from jax.experimental.pallas import tpu as pltpu
from jax.sharding import PartitionSpec as P

MESH = pl.DeviceIdType.MESH
F32 = jnp.float32
BF16 = jnp.bfloat16
CHUNKS = 4
LANES = 128
LOG2E = math.log2(math.e)


def dot_nn(a, b):
    return lax.dot_general(a, b, (((1,), (0,)), ((), ())), preferred_element_type=F32)


def dot_nt(a, b):
    return lax.dot_general(a, b, (((1,), (1,)), ((), ())), preferred_element_type=F32)


def folded(x):
    return jnp.sum(x.reshape(x.shape[0] // 8, 8, x.shape[1]), axis=0)


def peaked(x):
    return jnp.max(x.reshape(x.shape[0] // 8, 8, x.shape[1]), axis=0)


def lane_folded(x):
    parts = [x[:, at : at + LANES] for at in range(0, x.shape[1], LANES)]
    return functools.reduce(jnp.add, parts)


def wide(column, width):
    return jnp.concatenate([column] * (width // LANES), axis=1)


def kernel(
    peers, groups, w, c, g, gw, gc,
    e1, e2, ds, r1b, r2b, eb, sb, ct, mt, moved, mean, part, esum, column, den,
    stat_out, stat_in, row1, row2, cnt_out, cnt_in, mass_out, mass_in, mcot_out, mcot_in,
    start_out, start_in, own_moved, own_mean, own_start, start_all, grad_out, grad_in, own_grad,
    start_f, stat_send, stat_recv, send, recv, local,
):
    vectors, depth = w.shape
    cents = c.shape[0]
    block = vectors // groups
    share = cents // peers
    rows_of = cents // CHUNKS
    owners = peers // CHUNKS
    step = min(64, rows_of)
    vec = lax.axis_index("vec")
    cent = lax.axis_index("cent")
    scale = 2.0 * depth ** (-0.5)
    slope = 2.0 * depth ** (-0.5) * LOG2E
    offset = depth ** (-0.5) * LOG2E

    def along(axis, distance):
        if axis == "vec":
            return {"vec": lax.rem(vec + distance, peers)}
        return {"cent": lax.rem(cent + distance, groups)}

    def start(src, dst, sems, device):
        pltpu.make_async_remote_copy(
            src_ref=src, dst_ref=dst, send_sem=sems[0], recv_sem=sems[1],
            device_id=device, device_id_type=MESH,
        ).start()

    def wait_recv(ref, sem):
        pltpu.make_async_copy(ref, ref, sem).wait()

    def cols_of(j):
        return pl.ds(pl.multiple_of(j * block, block), block)

    def chunk_of(t):
        return lax.rem(vec // owners + t, CHUNKS)

    def rows_at(r):
        return pl.ds(pl.multiple_of(r * rows_of, rows_of), rows_of)

    barrier = pltpu.get_barrier_semaphore()
    for far in range(1, peers):
        pl.semaphore_signal(barrier, inc=1, device_id=along("vec", far), device_id_type=MESH)
    for far in range(1, groups):
        pl.semaphore_signal(barrier, inc=1, device_id=along("cent", far), device_id_type=MESH)

    def squares(ref):
        for at in range(0, cents, step):
            f = ref[at : at + step, :].astype(F32)
            total = jnp.sum(f * f, axis=1, keepdims=True) * offset
            sb[at : at + step, :] = jnp.broadcast_to(total, (step, block))

    def soften_block(cols, scores, cot):
        top = None
        for at in range(0, cents, step):
            here = peaked(scores[at : at + step, cols])
            top = here if top is None else jnp.maximum(top, here)
        top = jnp.max(top, axis=0, keepdims=True)
        total = dots = 0.0
        for at in range(0, cents, step):
            expo = jnp.exp2(scores[at : at + step, cols] - top)
            scores[at : at + step, cols] = expo
            total = total + folded(expo)
            if cot is not None:
                dots = dots + folded(expo * cot[at : at + step, cols])
        total = jnp.sum(total, axis=0, keepdims=True)
        if cot is None:
            return top, total, None
        return top, total, jnp.sum(dots, axis=0, keepdims=True)

    def send_stats(which, j, lines):
        for far in range(1, groups):
            start(
                stat_out.at[which, j, 0:lines],
                stat_in.at[which, j, groups - far, 0:lines],
                (stat_send, stat_recv.at[which, j]),
                along("cent", far),
            )

    def wait_stats(which, j, lines):
        ref = stat_in.at[which, j, 1:groups, 0:lines]
        wait_recv(ref, stat_recv.at[which, j])

    squares(c)
    pl.semaphore_wait(barrier, peers + groups - 2)

    def first_block(j, carry):
        cols = cols_of(j)
        cross = dot_nt(c[...], w[cols, :])
        for at in range(0, cents, step):
            e1[at : at + step, cols] = cross[at : at + step] * slope - sb[at : at + step, :]
        top, total, _ = soften_block(cols, e1, None)
        stat_out[0, j, 0:1, :] = top
        stat_out[0, j, 1:2, :] = total
        stat_in[0, j, 0, 0:1, :] = top
        stat_in[0, j, 0, 1:2, :] = total
        send_stats(0, j, 8)
        return carry

    lax.fori_loop(0, groups, first_block, 0)
    ct[...] = c[...].astype(F32).T.astype(BF16)

    def combine(which, j):
        peak = stat_in[which, j, 0, 0:1, :]
        for q in range(1, groups):
            peak = jnp.maximum(peak, stat_in[which, j, q, 0:1, :])
        total = dots = 0.0
        for q in range(groups):
            part_of = jnp.exp2(stat_in[which, j, q, 0:1, :] - peak)
            total = total + part_of * stat_in[which, j, q, 1:2, :]
            if which:
                dots = dots + part_of * stat_in[which, j, q, 2:3, :]
        mine = jnp.exp2(stat_in[which, j, 0, 0:1, :] - peak)
        return mine / total, dots / total

    def first_factor(j, carry):
        wait_stats(0, j, 8)
        row1[j, 0:1, :] = combine(0, j)[0]
        return carry

    lax.fori_loop(0, groups, first_factor, 0)

    def to_owners(r, which, out, arrived, extra=None):
        def one(q, carry):
            owner = r * owners + q
            far = lax.rem(owner - vec + peers, peers)
            slot = lax.rem(peers - far, peers)

            @pl.when(far != 0)
            def _():
                sems = (send.at[which], recv.at[which])
                start(out.at[owner], arrived.at[slot], sems, {"vec": owner})
                if extra is not None:
                    sems = (send.at[which + 1], recv.at[which + 1])
                    start(extra[0].at[r], extra[1].at[slot], sems, {"vec": owner})

            @pl.when(far == 0)
            def _():
                arrived[0] = out[owner]
                if extra is not None:
                    extra[1][0] = extra[0][r]

            return carry

        lax.fori_loop(0, owners, one, 0)

    def mass_chunk(t, carry):
        r = chunk_of(t)
        rows = rows_at(r)
        base = r * rows_of
        for at in range(0, rows_of, step):
            here = pl.ds(pl.multiple_of(base + at, step), step)
            count = 0.0
            for j in range(groups):
                cols = slice(j * block, (j + 1) * block)
                resp = e1[here, cols] * row1[j, 0:1, :]
                r1b[here, cols] = resp.astype(BF16)
                count = count + lane_folded(resp)
            count = jnp.sum(count, axis=1, keepdims=True)
            column[at : at + step, :] = jnp.broadcast_to(count, (step, LANES))
        cnt_out[r] = column[0:rows_of, :].T[0:1, :]
        mass = dot_nn(r1b[rows, :], w[...]).astype(BF16)
        for q in range(owners):
            mass_out[r * owners + q] = mass[q * share : (q + 1) * share]
        to_owners(r, 0, mass_out, mass_in, (cnt_out, cnt_in))
        return carry

    lax.fori_loop(0, CHUNKS, mass_chunk, 0)

    def wait_owners(which, arrived):
        wait_recv(arrived.at[1:peers], recv.at[which])

    def summed(arrived, count):
        total = arrived[0].astype(F32)
        for q in range(1, count):
            total = total + arrived[q].astype(F32)
        return total

    def to_all(which, own, everywhere):
        at = pl.ds(pl.multiple_of(vec * share, share), share)
        for far in range(1, peers):
            sems = (send.at[which], recv.at[which])
            start(own, everywhere.at[at, :], sems, along("vec", far))
        everywhere[at, :] = own[...]

    def wait_all(which, everywhere):
        wait_recv(everywhere.at[0 : (peers - 1) * share, :], recv.at[which])

    wait_owners(1, cnt_in)
    count = cnt_in[0]
    for q in range(1, peers):
        count = count + cnt_in[q]
    column[0:rows_of, :] = jnp.broadcast_to(count, (LANES, rows_of)).T
    mine = pl.ds(pl.multiple_of(lax.rem(vec, owners) * share, share), share)
    den[...] = column[mine, :] + 1e-6
    wait_owners(0, mass_in)
    own_moved[...] = (summed(mass_in, peers) / wide(den[...], depth)).astype(BF16)
    to_all(2, own_moved, moved)
    wait_all(2, moved)

    squares(moved)

    def second_block(j, carry):
        cols = cols_of(j)
        cross = dot_nt(moved[...], w[cols, :])
        for at in range(0, cents, step):
            e2[at : at + step, cols] = cross[at : at + step] * slope - sb[at : at + step, :]
        ds[:, cols] = dot_nt(moved[...], g[cols, :])
        top, total, dots = soften_block(cols, e2, ds)
        for line, value in enumerate((top, total, dots)):
            stat_out[1, j, line : line + 1, :] = value
            stat_in[1, j, 0, line : line + 1, :] = value
        send_stats(1, j, 8)
        return carry

    lax.fori_loop(0, groups, second_block, 0)
    mt[...] = moved[...].astype(F32).T.astype(BF16)

    def second_factor(j, carry):
        wait_stats(1, j, 8)
        factor, dots = combine(1, j)
        row2[j, 0:1, :] = factor
        row2[j, 1:2, :] = dots
        return carry

    lax.fori_loop(0, groups, second_factor, 0)

    def cot_chunk(t, carry):
        r = chunk_of(t)
        rows = rows_at(r)
        base = r * rows_of
        for at in range(0, rows_of, step):
            here = pl.ds(pl.multiple_of(base + at, step), step)
            total = 0.0
            for j in range(groups):
                cols = slice(j * block, (j + 1) * block)
                second = e2[here, cols] * row2[j, 0:1, :]
                r2b[here, cols] = second.astype(BF16)
                edge = second * (ds[here, cols] - row2[j, 1:2, :]) * scale
                eb[here, cols] = edge.astype(BF16)
                total = total + lane_folded(edge)
            total = jnp.sum(total, axis=1, keepdims=True)
            column[at : at + step, :] = jnp.broadcast_to(total, (step, LANES))
        cot = dot_nn(r2b[rows, :], g[...]) + dot_nn(eb[rows, :], w[...])
        for q in range(owners):
            inner = slice(q * share, (q + 1) * share)
            far = pl.ds(pl.multiple_of(base + q * share, share), share)
            value = cot[inner] - wide(column[inner, :], depth) * moved[far, :].astype(F32)
            mcot_out[r * owners + q] = value.astype(BF16)
        to_owners(r, 3, mcot_out, mcot_in)
        return carry

    lax.fori_loop(0, CHUNKS, cot_chunk, 0)

    def part_block(j, carry):
        cols = cols_of(j)
        part[:, cols] = dot_nn(mt[...], eb[:, cols])
        return carry

    lax.fori_loop(0, groups, part_block, 0)

    wait_owners(3, mcot_in)
    own_mean[...] = (summed(mcot_in, peers) / wide(den[...], depth)).astype(BF16)
    to_all(4, own_mean, mean)
    wait_all(4, mean)

    for at in range(0, cents, step):
        here = slice(at, at + step)
        total = jnp.sum(mean[here, :].astype(F32) * moved[here, :].astype(F32), axis=1, keepdims=True)
        sb[here, :] = jnp.broadcast_to(total, (step, block))

    def third_block(t, carry):
        j = lax.rem(cent + 1 + t, groups)
        cols = cols_of(j)
        cross = dot_nt(mean[...], w[cols, :])
        dots = 0.0
        for at in range(0, cents, step):
            dfirst = cross[at : at + step] - sb[at : at + step, :]
            ds[at : at + step, cols] = dfirst
            dots = dots + folded(e1[at : at + step, cols] * dfirst)
        dots = jnp.sum(dots, axis=0, keepdims=True) * row1[j, 0:1, :]
        stat_out[2, j, 0:1, :] = dots
        stat_in[2, j, 0, 0:1, :] = dots
        send_stats(2, j, 8)
        return carry

    lax.fori_loop(0, groups, third_block, 0)
    mt[...] = mean[...].astype(F32).T.astype(BF16)

    def grad_block(t, carry):
        j = lax.rem(cent + 1 + t, groups)
        cols = cols_of(j)
        wait_stats(2, j, 8)
        dots = stat_in[2, j, 0, 0:1, :]
        for q in range(1, groups):
            dots = dots + stat_in[2, j, q, 0:1, :]
        factor = row1[j, 0:1, :]
        for at in range(0, cents, step):
            first = e1[at : at + step, cols] * factor
            edge = first * (ds[at : at + step, cols] - dots) * scale
            eb[at : at + step, cols] = edge.astype(BF16)
            total = lane_folded(edge)

            @pl.when(t == 0)
            def _():
                esum[at : at + step, :] = total

            @pl.when(t != 0)
            def _():
                esum[at : at + step, :] += total

        grad = part[:, cols] + dot_nn(mt[...], r1b[:, cols]) + dot_nn(ct[...], eb[:, cols])
        grad_out[j] = grad.astype(BF16)

        @pl.when(t != groups - 1)
        def _():
            slot = lax.rem(cent - j + groups, groups)
            start(grad_out.at[j], grad_in.at[slot], (send.at[5], recv.at[5]), {"cent": j})

        @pl.when(t == groups - 1)
        def _():
            grad_in[0] = grad_out[j]

        return carry

    lax.fori_loop(0, groups, grad_block, 0)

    def start_chunk(t, carry):
        r = chunk_of(t)
        rows = rows_at(r)
        base = r * rows_of
        cot = dot_nn(eb[rows, :], w[...])
        for q in range(owners):
            inner = slice(q * share, (q + 1) * share)
            far = pl.ds(pl.multiple_of(base + q * share, share), share)
            total = jnp.sum(esum[far, :], axis=1, keepdims=True)
            value = cot[inner] - total * c[far, :].astype(F32)
            start_out[r * owners + q] = value.astype(BF16)
        to_owners(r, 6, start_out, start_in)
        return carry

    lax.fori_loop(0, CHUNKS, start_chunk, 0)

    wait_recv(grad_in.at[1:groups], recv.at[5])
    own_grad[...] = summed(grad_in, groups).T.astype(BF16)
    mine = pl.ds(pl.multiple_of(cent * block, block), block)
    for far in range(1, groups):
        start(own_grad, gw.at[mine, :], (send.at[7], recv.at[7]), along("cent", far))
    keep = pltpu.make_async_copy(own_grad, gw.at[mine, :], local.at[0])
    keep.start()

    wait_owners(6, start_in)
    own_start[...] = summed(start_in, peers).astype(BF16)
    to_all(8, own_start, start_all)
    wait_all(8, start_all)
    start_f[...] = start_all[...].astype(F32)
    result = pltpu.make_async_copy(start_f, gc, local.at[1])
    result.start()
    wait_recv(gw.at[0 : (groups - 1) * block, :], recv.at[7])
    keep.wait()
    result.wait()

    wait_recv(stat_in.at[:, :, 1:groups], stat_send)
    wait_recv(mass_in.at[1:peers], send.at[0])
    wait_recv(cnt_in.at[1:peers], send.at[1])
    wait_recv(mcot_in.at[1:peers], send.at[3])
    wait_recv(start_in.at[1:peers], send.at[6])
    wait_recv(grad_in.at[1:groups], send.at[5])
    wait_recv(gw.at[0 : (groups - 1) * block, :], send.at[7])
    for which, ref in ((2, moved), (4, mean), (8, start_all)):
        wait_recv(ref.at[0 : (peers - 1) * share, :], send.at[which])


def body(peers, groups, weights, centroids, cotangent):
    vectors, depth = weights.shape
    cents = centroids.shape[0]
    block = vectors // groups
    share = cents // peers
    rows_of = cents // CHUNKS
    vmem = pltpu.VMEM
    scratch = [
        vmem((cents, vectors), F32),
        vmem((cents, vectors), F32),
        vmem((cents, vectors), F32),
        vmem((cents, vectors), BF16),
        vmem((cents, vectors), BF16),
        vmem((cents, vectors), BF16),
        vmem((cents, block), F32),
        vmem((depth, cents), BF16),
        vmem((depth, cents), BF16),
        vmem((cents, depth), BF16),
        vmem((cents, depth), BF16),
        vmem((depth, vectors), F32),
        vmem((cents, LANES), F32),
        vmem((rows_of, LANES), F32),
        vmem((share, LANES), F32),
        vmem((3, groups, 8, block), F32),
        vmem((3, groups, groups, 8, block), F32),
        vmem((groups, 8, block), F32),
        vmem((groups, 8, block), F32),
        vmem((CHUNKS, 1, rows_of), F32),
        vmem((peers, 1, rows_of), F32),
        vmem((peers, share, depth), BF16),
        vmem((peers, share, depth), BF16),
        vmem((peers, share, depth), BF16),
        vmem((peers, share, depth), BF16),
        vmem((peers, share, depth), BF16),
        vmem((peers, share, depth), BF16),
        vmem((share, depth), BF16),
        vmem((share, depth), BF16),
        vmem((share, depth), BF16),
        vmem((cents, depth), BF16),
        vmem((groups, depth, block), BF16),
        vmem((groups, depth, block), BF16),
        vmem((block, depth), BF16),
        vmem((cents, depth), F32),
        pltpu.SemaphoreType.DMA,
        pltpu.SemaphoreType.DMA((3, groups)),
        pltpu.SemaphoreType.DMA((9,)),
        pltpu.SemaphoreType.DMA((9,)),
        pltpu.SemaphoreType.DMA((2,)),
    ]
    return pl.pallas_call(
        functools.partial(kernel, peers, groups),
        out_shape=(
            jax.ShapeDtypeStruct((vectors, depth), BF16),
            jax.ShapeDtypeStruct((cents, depth), F32),
        ),
        in_specs=[pl.BlockSpec(memory_space=pltpu.VMEM)] * 3,
        out_specs=[pl.BlockSpec(memory_space=pl.ANY)] * 2,
        scratch_shapes=scratch,
        compiler_params=pltpu.CompilerParams(
            collective_id=0, has_side_effects=True, vmem_limit_bytes=67043328
        ),
        name="soft_assignments",
    )(weights, centroids, cotangent)


def solution(mesh):
    return jax.shard_map(
        functools.partial(body, mesh.shape["vec"], mesh.shape["cent"]),
        mesh=mesh,
        in_specs=(P("vec", None), P("cent", None), P("vec", None)),
        out_specs=(P("vec", None), P("cent", None)),
        check_vma=False,
    )
```

time: 334 us -> 120 us (0.36)
  Pallas kernels: 0 us -> 115 us
  blocking collectives: 115 us -> 0 us
  waiting for transfers between devices: 93.6 us -> 0 us
  matrix products: 46.8 us -> 0 us
  other arithmetic: 28.9 us -> 0 us
  starting transfers between devices: 17.5 us -> 0 us
  between operations: 15.1 us -> 0.65 us
  local copies, waits for them, and re-layouts: 14.8 us -> 3.32 us
    pallas_call x0 -> x1, Pallas kernels: none -> 115 us  [body(): pl.pallas_call(functools.partial(kernel, peers, groups), out_shape=(jax.S...]
    all_to_all x5 -> x0, blocking collectives: 67.8 us -> none  [the longest x4 54.3 us: from_everyone(): lax.all_to_all(jnp.broadcast_to(value[None], (peers, *value.shape)), axis...]
    reduce_scatter x2 -> x0, waiting for transfers between devices: 64.4 us -> none  [the longest x1 34.1 us: total_of(): lax.psum_scatter(filled_up(lines, lax.axis_size(axis)), axis, scatter_dim...]
    dot_general x11 -> x0, matrix products: 46.8 us -> none  [the longest x1 7.89 us: body(): jnp.dot(weights, mean_cot.T, preferred_element_type=jnp.float32)]
    all_to_all x4 -> x0, waiting for transfers between devices: 29.2 us -> none  [the longest x1 22.3 us: sent_and_summed_2(): tiles = lax.all_to_all(in_blocks(value, dim, peers), axis, 0, 0, tiled=True)]
    unnamed x1 -> x0, blocking collectives: 28.2 us -> none
    reduce_sum x12 -> x0, other arithmetic: 26.5 us -> none  [the longest x1 7.67 us: body(): moved_cot = moved_cot - jnp.sum(edge_two, axis=0)[:, None] * moved_f]
    all_gather x1 -> x0, blocking collectives: 19 us -> none  [total_of(): whole = lax.all_gather(own, axis).reshape(-1, *lines.shape[1:])]
  transfers between devices with their start and end apart: 6 -> 0, of which waited for: 5 -> 0; matrix products, arithmetic and copies ran while one was open for 6% -> 0% of each run, Pallas kernels for 0% -> 0%
where the time goes in v1:
time: 120 us; the launch traced here: 119 us
  Pallas kernels  115 us (96%)
  local copies, waits for them, and re-layouts  3.32 us (3%)
    pallas_call x1, Pallas kernels, body(): pl.pallas_call(functools.partial(kernel, peers, groups), out_shape=(jax.S...  115 us
    unnamed x4, local copies, waits for them, and re-layouts  3.32 us

profile of v1, /device:TPU:0, one launch (start us, length us, event | category | flops | bytes accessed | tf_op | source)
XLA Modules:
  0.0 118.8 jit_solution(16475445414830434994)
XLA Ops:
  0.6 114.8 %soft_assignments.1 = (bf16[2048,256]{1,0:T(8,128)(2,1)}, f32[1024,256]{1,0:T(8,128)}) custom-call(bf16[2048,256]{1,0:T(8,128)(2,1)} %w.1, bf16[1024,256]{1,0:T(8,128)(2,1)} %c.1, bf16[2048,256]{1,0:T(8,128)(2,1)} %g.1), custom_call_target="tpu_custom_call" | custom-call | tf_op jit(solution)/shard_map/soft_assignments/pallas_call | solution.py:469
  115.5 0.0 copy-start
  115.5 2.4 %copy.7 = bf16[2048,256]{1,0:T(8,128)(2,1)} copy(bf16[2048,256]{1,0:T(8,128)(2,1)} %get-tuple-element.4) | data formatting | bytes 2097152
  117.8 0.0 copy-done
  117.8 1.0 copy.8
Async XLA Ops:
  115.5 2.4 %copy-start = (f32[1024,256]{1,0:T(8,128)S(1)}, f32[1024,256]{1,0:T(8,128)}, u32[]{:S(2)}) copy-start(f32[1024,256]{1,0:T(8,128)} %get-tuple-element.5) | copy-start | bytes 3145732

commit v2 on v1

v2 whole, which is shorter than its diff:
```python
import functools
import math

import jax
import jax.numpy as jnp
from jax import lax
from jax.experimental import pallas as pl
from jax.experimental.pallas import tpu as pltpu
from jax.sharding import PartitionSpec as P

MESH = pl.DeviceIdType.MESH
F32 = jnp.float32
BF16 = jnp.bfloat16
CORES = 2
PAIR = 2
STATS = (2, 3, 1)
LANES = 128
LOG2E = math.log2(math.e)


def dot_nn(a, b):
    return lax.dot_general(a, b, (((1,), (0,)), ((), ())), preferred_element_type=F32)


def dot_nt(a, b):
    return lax.dot_general(a, b, (((1,), (1,)), ((), ())), preferred_element_type=F32)


def folded(x):
    return jnp.sum(x.reshape(x.shape[0] // 8, 8, x.shape[1]), axis=0)


def peaked(x):
    return jnp.max(x.reshape(x.shape[0] // 8, 8, x.shape[1]), axis=0)


def lane_folded(x):
    parts = [x[:, at : at + LANES] for at in range(0, x.shape[1], LANES)]
    return functools.reduce(jnp.add, parts)


def wide(column, width):
    return jnp.concatenate([column] * (width // LANES), axis=1)


def kernel(
    peers, groups, w, c, g, gw, gc,
    e1, e2, ds, r1b, r2b, eb, sb, ct, mt, moved, mean, part, esum, column, den,
    stat_out, stat_in, row1, row2, cnt_out, cnt_near, cnt_both, cnt_in, near_out, near_in, sum_out, sum_in,
    own_moved, own_mean, own_start, start_all, grad_out, grad_in, pair_keep, pair_out, pair_in, own_grad,
    stat_send, stat_recv, near_send, near_recv, cnt_send, cnt_recv, sum_send, sum_recv, all_send, all_recv,
    both_send, both_recv, grad_send, grad_recv, pair_send, pair_recv, out_send, out_recv, local,
):
    vectors, depth = w.shape
    cents = c.shape[0]
    block = vectors // groups
    half = vectors // 2
    piece = half // groups
    share = cents // peers
    chips = peers // CORES
    ring_y = chips // PAIR
    ring_z = groups // PAIR
    rows_of = cents // ring_y
    owners = PAIR * CORES
    step = min(64, rows_of)
    vec = lax.axis_index("vec")
    cent = lax.axis_index("cent")
    chip, core = vec // CORES, lax.rem(vec, CORES)
    y, x_low = chip // PAIR, lax.rem(chip, PAIR)
    x_high, z = cent // ring_z, lax.rem(cent, ring_z)
    sibling = {"vec": vec + 1 - 2 * core}
    scale = 2.0 * depth ** (-0.5)
    slope = 2.0 * depth ** (-0.5) * LOG2E
    offset = depth ** (-0.5) * LOG2E

    def start(src, dst, send, recv, device):
        pltpu.make_async_remote_copy(
            src_ref=src, dst_ref=dst, send_sem=send, recv_sem=recv,
            device_id=device, device_id_type=MESH,
        ).start()

    def wait(ref, sem):
        pltpu.make_async_copy(ref, ref, sem).wait()

    def cent_at(far):
        return {"cent": lax.rem(cent + far, groups)}

    def chip_at(far):
        return lax.rem(chip + far, chips)

    def cols_of(j):
        return pl.ds(pl.multiple_of(j * block, block), block)

    def chunk_of(t):
        return lax.rem(y + 1 + t, ring_y)

    def rows_at(r):
        return pl.ds(pl.multiple_of(r * rows_of, rows_of), rows_of)

    def rows_from(owner):
        return pl.ds(pl.multiple_of(owner * share, share), share)

    barrier = pltpu.get_barrier_semaphore()
    pl.semaphore_signal(barrier, inc=1, device_id=sibling, device_id_type=MESH)
    for far in range(1, chips):
        there = {"vec": chip_at(far) * CORES + core}
        pl.semaphore_signal(barrier, inc=1, device_id=there, device_id_type=MESH)
    for far in range(1, groups):
        pl.semaphore_signal(barrier, inc=1, device_id=cent_at(far), device_id_type=MESH)

    def squares(ref):
        for at in range(0, cents, step):
            f = ref[at : at + step, :].astype(F32)
            total = jnp.sum(f * f, axis=1, keepdims=True) * offset
            sb[at : at + step, :] = jnp.broadcast_to(total, (step, block))

    def soften_block(cols, scores, cot):
        top = None
        for at in range(0, cents, step):
            here = peaked(scores[at : at + step, cols])
            top = here if top is None else jnp.maximum(top, here)
        top = jnp.max(top, axis=0, keepdims=True)
        total = dots = 0.0
        for at in range(0, cents, step):
            expo = jnp.exp2(scores[at : at + step, cols] - top)
            scores[at : at + step, cols] = expo
            total = total + folded(expo)
            if cot is not None:
                dots = dots + folded(expo * cot[at : at + step, cols])
        total = jnp.sum(total, axis=0, keepdims=True)
        if cot is None:
            return top, total
        return top, total, jnp.sum(dots, axis=0, keepdims=True)

    def send_stats(which, j, values):
        lanes = slice(0, len(values) * block)
        for line, value in enumerate(values):
            inner = slice(line * block, (line + 1) * block)
            stat_out[which, j, :, inner] = value
            stat_in[which, j, 0, :, inner] = value
        for far in range(1, groups):
            start(
                stat_out.at[which, j, :, lanes],
                stat_in.at[which, j, groups - far, :, lanes],
                stat_send.at[which],
                stat_recv.at[which, j],
                cent_at(far),
            )

    def wait_stats(which, j):
        lanes = slice(0, STATS[which] * block)
        wait(stat_in.at[which, j, 1:groups, :, lanes], stat_recv.at[which, j])

    def stat(which, j, q, line):
        return stat_in[which, j, q, :, line * block : (line + 1) * block]

    squares(c)
    pl.semaphore_wait(barrier, chips + groups - 1)

    def first_block(j, carry):
        cols = cols_of(j)
        cross = dot_nt(c[...], w[cols, :])
        for at in range(0, cents, step):
            e1[at : at + step, cols] = cross[at : at + step] * slope - sb[at : at + step, :]
        send_stats(0, j, soften_block(cols, e1, None))
        return carry

    lax.fori_loop(0, groups, first_block, 0)
    ct[...] = c[...].astype(F32).T.astype(BF16)

    def combine(which, j):
        peak = stat(which, j, 0, 0)
        for q in range(1, groups):
            peak = jnp.maximum(peak, stat(which, j, q, 0))
        total = dots = 0.0
        for q in range(groups):
            part_of = jnp.exp2(stat(which, j, q, 0) - peak)
            total = total + part_of * stat(which, j, q, 1)
            if STATS[which] > 2:
                dots = dots + part_of * stat(which, j, q, 2)
        mine = jnp.exp2(stat(which, j, 0, 0) - peak)
        return mine / total, dots / total

    def first_factor(j, carry):
        wait_stats(0, j)
        row1[j, 0:1, :] = combine(0, j)[0]
        return carry

    lax.fori_loop(0, groups, first_factor, 0)

    def to_sibling(which, r, value):
        for q in range(owners):
            near_out[which, r, q] = value[q * share : (q + 1) * share]
        for q in range(PAIR):
            theirs = q * CORES + 1 - core
            start(
                near_out.at[which, r, theirs],
                near_in.at[which, r, q],
                near_send.at[which],
                near_recv.at[which, r],
                sibling,
            )

    def to_owners(which, r):
        wait(near_in.at[which, r], near_recv.at[which, r])
        if which == 0:
            wait(cnt_near.at[r], cnt_recv.at[r])
            cnt_both[r] = cnt_out[r] + cnt_near[r]

        def one(q, carry):
            total = near_out[which, r, q * CORES + core] + near_in[which, r, q]
            there = r * PAIR + q
            far = lax.rem(there - chip + chips, chips)
            slot = lax.rem(chips - far, chips)
            sum_out[which, there] = total.astype(BF16)

            @pl.when(far != 0)
            def _():
                device = {"vec": there * CORES + core}
                start(
                    sum_out.at[which, there], sum_in.at[which, slot],
                    sum_send.at[which], sum_recv.at[which], device,
                )
                if which == 0:
                    start(
                        cnt_both.at[r], cnt_in.at[slot],
                        cnt_send.at[1], cnt_recv.at[ring_y], device,
                    )

            @pl.when(far == 0)
            def _():
                sum_in[which, 0] = total.astype(BF16)
                if which == 0:
                    cnt_in[0] = cnt_both[r]

            return carry

        lax.fori_loop(0, PAIR, one, 0)

    def by_chunks(which, chunk):
        def one(t, carry):
            chunk(chunk_of(t))

            @pl.when(t > 0)
            def _():
                to_owners(which, chunk_of(t - 1))

            return carry

        lax.fori_loop(0, ring_y, one, 0)
        to_owners(which, chunk_of(ring_y - 1))

    def summed_up(which):
        wait(sum_in.at[which, 1:chips], sum_recv.at[which])
        total = sum_in[which, 0].astype(F32)
        for q in range(1, chips):
            total = total + sum_in[which, q].astype(F32)
        return total

    def to_all(which, own, everywhere):
        at = rows_from(vec)
        for far in range(1, chips):
            start(
                own, everywhere.at[at, :],
                all_send.at[which], all_recv.at[which, chips - far],
                {"vec": chip_at(far) * CORES + core},
            )
        start(own, everywhere.at[at, :], both_send.at[which], both_recv.at[which], sibling)
        everywhere[at, :] = own[...]

    def wait_all(which, everywhere):
        for k in range(1, chips):
            far = (k + 1) // 2 if k % 2 else chips - k // 2
            at = rows_from(chip_at(far) * CORES + core)
            wait(everywhere.at[at, :], all_recv.at[which, far])
            start(
                everywhere.at[at, :], everywhere.at[at, :],
                both_send.at[which], both_recv.at[which], sibling,
            )
        wait(everywhere.at[0 : chips * share, :], both_recv.at[which])

    def mass_chunk(r):
        base = r * rows_of
        for at in range(0, rows_of, step):
            here = pl.ds(pl.multiple_of(base + at, step), step)
            count = 0.0
            for j in range(groups):
                cols = slice(j * block, (j + 1) * block)
                resp = e1[here, cols] * row1[j, 0:1, :]
                r1b[here, cols] = resp.astype(BF16)
                count = count + lane_folded(resp)
            count = jnp.sum(count, axis=1, keepdims=True)
            column[at : at + step, :] = jnp.broadcast_to(count, (step, LANES))
        cnt_out[r] = column[...].T[0:1, :]
        to_sibling(0, r, dot_nn(r1b[rows_at(r), :], w[...]))
        start(cnt_out.at[r], cnt_near.at[r], cnt_send.at[0], cnt_recv.at[r], sibling)

    by_chunks(0, mass_chunk)

    wait(cnt_in.at[1:chips], cnt_recv.at[ring_y])
    count = cnt_in[0]
    for q in range(1, chips):
        count = count + cnt_in[q]
    column[...] = jnp.broadcast_to(count, (LANES, rows_of)).T
    den[...] = column[rows_from(lax.rem(vec, owners)), :] + 1e-6
    own_moved[...] = (summed_up(0) / wide(den[...], depth)).astype(BF16)
    to_all(0, own_moved, moved)
    wait_all(0, moved)

    squares(moved)

    def second_block(j, carry):
        cols = cols_of(j)
        cross = dot_nt(moved[...], w[cols, :])
        for at in range(0, cents, step):
            e2[at : at + step, cols] = cross[at : at + step] * slope - sb[at : at + step, :]
        ds[:, cols] = dot_nt(moved[...], g[cols, :])
        send_stats(1, j, soften_block(cols, e2, ds))
        return carry

    lax.fori_loop(0, groups, second_block, 0)
    mt[...] = moved[...].astype(F32).T.astype(BF16)

    def second_factor(j, carry):
        wait_stats(1, j)
        factor, dots = combine(1, j)
        row2[j, 0:1, :] = factor
        row2[j, 1:2, :] = dots
        return carry

    lax.fori_loop(0, groups, second_factor, 0)

    def cot_chunk(r):
        base = r * rows_of
        rows = rows_at(r)
        for at in range(0, rows_of, step):
            here = pl.ds(pl.multiple_of(base + at, step), step)
            total = 0.0
            for j in range(groups):
                cols = slice(j * block, (j + 1) * block)
                second = e2[here, cols] * row2[j, 0:1, :]
                r2b[here, cols] = second.astype(BF16)
                edge = second * (ds[here, cols] - row2[j, 1:2, :]) * scale
                eb[here, cols] = edge.astype(BF16)
                total = total + lane_folded(edge)
            total = jnp.sum(total, axis=1, keepdims=True)
            column[at : at + step, :] = jnp.broadcast_to(total, (step, LANES))
        cot = dot_nn(r2b[rows, :], g[...]) + dot_nn(eb[rows, :], w[...])
        to_sibling(1, r, cot - wide(column[...], depth) * moved[rows, :].astype(F32))

    by_chunks(1, cot_chunk)

    def part_block(j, carry):
        cols = cols_of(j)
        part[:, cols] = dot_nn(mt[...], eb[:, cols])
        return carry

    lax.fori_loop(0, groups, part_block, 0)

    own_mean[...] = (summed_up(1) / wide(den[...], depth)).astype(BF16)
    to_all(1, own_mean, mean)
    wait_all(1, mean)

    for at in range(0, cents, step):
        here = slice(at, at + step)
        total = jnp.sum(mean[here, :].astype(F32) * moved[here, :].astype(F32), axis=1, keepdims=True)
        sb[here, :] = jnp.broadcast_to(total, (step, block))

    in_half = groups // 2

    def block_at(u):
        h, t = u // in_half, lax.rem(u, in_half)
        far_x = lax.rem(t, PAIR)
        two_z = lax.rem(z // 2 + 1 + t // PAIR, ring_z // 2)
        return h, h * in_half + far_x * (ring_z // 2) + two_z, far_x, two_z * 2

    def third_block(u, carry):
        j = block_at(u)[1]
        cols = cols_of(j)
        cross = dot_nt(mean[...], w[cols, :])
        dots = 0.0
        for at in range(0, cents, step):
            dfirst = cross[at : at + step] - sb[at : at + step, :]
            ds[at : at + step, cols] = dfirst
            dots = dots + folded(e1[at : at + step, cols] * dfirst)
        send_stats(2, j, (jnp.sum(dots, axis=0, keepdims=True) * row1[j, 0:1, :],))
        return carry

    lax.fori_loop(0, groups, third_block, 0)
    mt[...] = mean[...].astype(F32).T.astype(BF16)

    def grad_block(u, carry):
        h, j, to_x, first_z = block_at(u)
        cols = cols_of(j)
        wait_stats(2, j)
        dots = stat(2, j, 0, 0)
        for q in range(1, groups):
            dots = dots + stat(2, j, q, 0)
        factor = row1[j, 0:1, :]
        for at in range(0, cents, step):
            first = e1[at : at + step, cols] * factor
            edge = first * (ds[at : at + step, cols] - dots) * scale
            eb[at : at + step, cols] = edge.astype(BF16)
            total = lane_folded(edge)

            @pl.when(u == 0)
            def _():
                esum[at : at + step, :] = total

            @pl.when(u != 0)
            def _():
                esum[at : at + step, :] += total

        grad = part[:, cols] + dot_nn(mt[...], r1b[:, cols]) + dot_nn(ct[...], eb[:, cols])
        grad = grad.astype(BF16)
        for q in range(2):
            to_z = first_z + q
            far = lax.rem(to_z - z + ring_z, ring_z)
            slot = lax.rem(ring_z - far, ring_z)
            mine = grad[:, q * piece : (q + 1) * piece]
            grad_out[h, to_x, to_z] = mine

            @pl.when(far != 0)
            def _():
                start(
                    grad_out.at[h, to_x, to_z], grad_in.at[h, slot, to_x],
                    grad_send, grad_recv.at[h], {"cent": x_high * ring_z + to_z},
                )

            @pl.when(far == 0)
            def _():
                grad_in[h, 0, to_x] = mine

        return carry

    lax.fori_loop(0, groups, grad_block, 0)

    other = {"cent": (1 - x_high) * ring_z + z}

    def over_z(h):
        wait(grad_in.at[h, 1:ring_z], grad_recv.at[h])

        def total(to_x):
            value = grad_in[h, 0, to_x].astype(F32)
            for q in range(1, ring_z):
                value = value + grad_in[h, q, to_x].astype(F32)
            return value

        pair_out[h] = total(1 - x_high).astype(BF16)
        start(pair_out.at[h], pair_in.at[h], pair_send, pair_recv.at[h], other)
        pair_keep[h] = total(x_high)

    def over_x(h):
        wait(pair_in.at[h], pair_recv.at[h])
        total = pair_keep[h] + pair_in[h].astype(F32)
        own_grad[h] = total.T.astype(BF16)
        rows = pl.ds(pl.multiple_of(h * half + cent * piece, piece), piece)
        for far in range(1, groups):
            start(own_grad.at[h], gw.at[rows, :], out_send, out_recv, cent_at(far))
        pltpu.make_async_copy(own_grad.at[h], gw.at[rows, :], local.at[h]).start()

    def start_chunk(r):
        rows = rows_at(r)
        total = jnp.sum(esum[rows, :], axis=1, keepdims=True)
        value = dot_nn(eb[rows, :], w[...]) - total * c[rows, :].astype(F32)
        to_sibling(2, r, value)

    over_z(0)
    by_chunks(2, start_chunk)
    over_x(0)
    over_z(1)
    own_start[...] = summed_up(2).astype(BF16)
    to_all(2, own_start, start_all)
    over_x(1)
    wait_all(2, start_all)
    result = pltpu.make_async_copy(start_all, gc, local.at[2])
    result.start()
    wait(gw.at[0 : (groups - 1) * 2 * piece, :], out_recv)
    for h in range(2):
        pltpu.make_async_copy(own_grad.at[h], gw.at[0:piece, :], local.at[h]).wait()
    result.wait()

    for which in range(3):
        lanes = slice(0, STATS[which] * block)
        wait(stat_in.at[which, :, 1:groups, :, lanes], stat_send.at[which])
        wait(near_in.at[which], near_send.at[which])
        wait(sum_in.at[which, 1:chips], sum_send.at[which])
        wait(start_all.at[0 : (chips - 1) * share, :], all_send.at[which])
        wait(start_all.at[0 : chips * share, :], both_send.at[which])
    wait(cnt_near, cnt_send.at[0])
    wait(cnt_in.at[1:chips], cnt_send.at[1])
    wait(grad_in.at[:, 1:ring_z], grad_send)
    wait(pair_in, pair_send)
    wait(gw.at[0 : (groups - 1) * 2 * piece, :], out_send)


def body(peers, groups, weights, centroids, cotangent):
    vectors, depth = weights.shape
    cents = centroids.shape[0]
    block = vectors // groups
    piece = vectors // 2 // groups
    share = cents // peers
    chips = peers // CORES
    ring_y = chips // PAIR
    ring_z = groups // PAIR
    rows_of = cents // ring_y
    owners = PAIR * CORES
    vmem = pltpu.VMEM
    dma = pltpu.SemaphoreType.DMA
    scratch = [
        vmem((cents, vectors), F32),
        vmem((cents, vectors), F32),
        vmem((cents, vectors), F32),
        vmem((cents, vectors), BF16),
        vmem((cents, vectors), BF16),
        vmem((cents, vectors), BF16),
        vmem((cents, block), F32),
        vmem((depth, cents), BF16),
        vmem((depth, cents), BF16),
        vmem((cents, depth), BF16),
        vmem((cents, depth), BF16),
        vmem((depth, vectors), F32),
        vmem((cents, LANES), F32),
        vmem((rows_of, LANES), F32),
        vmem((share, LANES), F32),
        vmem((3, groups, 1, 3 * block), F32),
        vmem((3, groups, groups, 1, 3 * block), F32),
        vmem((groups, 8, block), F32),
        vmem((groups, 8, block), F32),
        vmem((ring_y, 1, rows_of), F32),
        vmem((ring_y, 1, rows_of), F32),
        vmem((ring_y, 1, rows_of), F32),
        vmem((chips, 1, rows_of), F32),
        vmem((3, ring_y, owners, share, depth), F32),
        vmem((3, ring_y, PAIR, share, depth), F32),
        vmem((3, chips, share, depth), BF16),
        vmem((3, chips, share, depth), BF16),
        vmem((share, depth), BF16),
        vmem((share, depth), BF16),
        vmem((share, depth), BF16),
        vmem((cents, depth), BF16),
        vmem((2, PAIR, ring_z, depth, piece), BF16),
        vmem((2, ring_z, PAIR, depth, piece), BF16),
        vmem((2, depth, piece), F32),
        vmem((2, depth, piece), BF16),
        vmem((2, depth, piece), BF16),
        vmem((2, piece, depth), BF16),
        dma((3,)),
        dma((3, groups)),
        dma((3,)),
        dma((3, ring_y)),
        dma((2,)),
        dma((ring_y + 1,)),
        dma((3,)),
        dma((3,)),
        dma((3,)),
        dma((3, chips)),
        dma((3,)),
        dma((3,)),
        dma,
        dma((2,)),
        dma,
        dma((2,)),
        dma,
        dma,
        dma((3,)),
    ]
    grad_rows, start_cot = pl.pallas_call(
        functools.partial(kernel, peers, groups),
        out_shape=(
            jax.ShapeDtypeStruct((vectors, depth), BF16),
            jax.ShapeDtypeStruct((cents, depth), BF16),
        ),
        in_specs=[pl.BlockSpec(memory_space=pltpu.VMEM)] * 3,
        out_specs=[pl.BlockSpec(memory_space=pl.ANY)] * 2,
        scratch_shapes=scratch,
        compiler_params=pltpu.CompilerParams(
            collective_id=0, has_side_effects=True, vmem_limit_bytes=67043328
        ),
        name="soft_assignments",
    )(weights, centroids, cotangent)
    return grad_rows, start_cot.astype(F32)


def solution(mesh):
    return jax.shard_map(
        functools.partial(body, mesh.shape["vec"], mesh.shape["cent"]),
        mesh=mesh,
        in_specs=(P("vec", None), P("cent", None), P("vec", None)),
        out_specs=(P("vec", None), P("cent", None)),
        check_vma=False,
    )
```

time: 120 us -> 101 us (0.84)
  Pallas kernels: 115 us -> 97.1 us
  local copies, waits for them, and re-layouts: 3.32 us -> 0.97 us
  other arithmetic: 0 us -> 2.17 us
    pallas_call x1, Pallas kernels: 115 us -> 97.1 us  [body(): pl.pallas_call(functools.partial(kernel, peers, groups), out_shape=(jax.S...]
    unnamed x4 -> x3, local copies, waits for them, and re-layouts: 3.32 us -> 0.97 us
    convert_element_type x0 -> x1, other arithmetic: none -> 2.17 us  [body(): return (grad_rows, start_cot.astype(F32))]
where the time goes in v2:
time: 101 us
  Pallas kernels  97.1 us (96%)
  other arithmetic  2.17 us (2%)
    pallas_call x1, Pallas kernels, body(): pl.pallas_call(functools.partial(kernel, peers, groups), out_shape=(jax.S...  97.1 us
    convert_element_type x1, other arithmetic, body(): return (grad_rows, start_cot.astype(F32))  2.17 us

profile of v2, /device:TPU:0, one launch (start us, length us, event | category | flops | bytes accessed | tf_op | source)
XLA Modules:
  0.0 100.9 jit_solution(3526622280423761028)
XLA Ops:
  0.6 97.1 %soft_assignments.1 = (bf16[2048,256]{1,0:T(8,128)(2,1)}, bf16[1024,256]{1,0:T(8,128)(2,1)}) custom-call(bf16[2048,256]{1,0:T(8,128)(2,1)} %w.1, bf16[1024,256]{1,0:T(8,128)(2,1)} %c.1, bf16[2048,256]{1,0:T(8,128)(2,1)} %g.1), custom_call_target="tpu_custom_call" | custom-call | tf_op jit(solution)/shard_map/soft_assignments/pallas_call | solution.py:568
  97.8 0.0 copy-start
  97.8 2.2 %convert_element_type.3 = f32[1024,256]{1,0:T(8,128)} convert(bf16[1024,256]{1,0:T(8,128)(2,1)} %get-tuple-element.5) | non-fusion elementwise | flops 262144 | bytes 1572864 | tf_op jit(solution)/shard_map/convert_element_type | solution.py:582
  99.9 0.0 copy-done
  99.9 1.0 copy.6
Async XLA Ops:
  97.8 2.2 %copy-start = (bf16[2048,256]{1,0:T(8,128)(2,1)S(1)}, bf16[2048,256]{1,0:T(8,128)(2,1)}, u32[]{:S(2)}) copy-start(bf16[2048,256]{1,0:T(8,128)(2,1)} %get-tuple-element.8) | copy-start | bytes 3145732

commit v3 on v2

--- a/solution.py
+++ b/solution.py
@@ -44,7 +44,8 @@
 
 
 def kernel(
-    peers, groups, w, c, g, gw, gc,
+    peers, groups, w_hbm, c_hbm, g_hbm, gw, gc,
+    w, c, g, top_acc,
     e1, e2, ds, r1b, r2b, eb, sb, ct, mt, moved, mean, part, esum, column, den,
     stat_out, stat_in, row1, row2, cnt_out, cnt_near, cnt_both, cnt_in, near_out, near_in, sum_out, sum_in,
     own_moved, own_mean, own_start, start_all, grad_out, grad_in, pair_keep, pair_out, pair_in, own_grad,
@@ -100,6 +101,13 @@
     def rows_from(owner):
         return pl.ds(pl.multiple_of(owner * share, share), share)
 
+    loads = [
+        pltpu.make_async_copy(src, dst, local.at[3 + n])
+        for n, (src, dst) in enumerate(((c_hbm, c), (w_hbm, w), (g_hbm, g)))
+    ]
+    for load in loads:
+        load.start()
+
     barrier = pltpu.get_barrier_semaphore()
     pl.semaphore_signal(barrier, inc=1, device_id=sibling, device_id_type=MESH)
     for far in range(1, chips):
@@ -108,18 +116,7 @@
     for far in range(1, groups):
         pl.semaphore_signal(barrier, inc=1, device_id=cent_at(far), device_id_type=MESH)
 
-    def squares(ref):
-        for at in range(0, cents, step):
-            f = ref[at : at + step, :].astype(F32)
-            total = jnp.sum(f * f, axis=1, keepdims=True) * offset
-            sb[at : at + step, :] = jnp.broadcast_to(total, (step, block))
-
-    def soften_block(cols, scores, cot):
-        top = None
-        for at in range(0, cents, step):
-            here = peaked(scores[at : at + step, cols])
-            top = here if top is None else jnp.maximum(top, here)
-        top = jnp.max(top, axis=0, keepdims=True)
+    def expo_block(cols, top, scores, cot):
         total = dots = 0.0
         for at in range(0, cents, step):
             expo = jnp.exp2(scores[at : at + step, cols] - top)
@@ -154,18 +151,32 @@
     def stat(which, j, q, line):
         return stat_in[which, j, q, :, line * block : (line + 1) * block]
 
-    squares(c)
-    pl.semaphore_wait(barrier, chips + groups - 1)
-
-    def first_block(j, carry):
-        cols = cols_of(j)
+    loads[0].wait()
+    for at in range(0, cents, step):
+        f = c[at : at + step, :].astype(F32)
+        total = jnp.sum(f * f, axis=1, keepdims=True) * offset
+        sb[at : at + step, :] = jnp.broadcast_to(total, (step, block))
+    loads[1].wait()
+
+    def first_scores(j):
+        cols = slice(j * block, (j + 1) * block)
         cross = dot_nt(c[...], w[cols, :])
+        top = None
         for at in range(0, cents, step):
-            e1[at : at + step, cols] = cross[at : at + step] * slope - sb[at : at + step, :]
-        send_stats(0, j, soften_block(cols, e1, None))
-        return carry
-
-    lax.fori_loop(0, groups, first_block, 0)
+            score = cross[at : at + step] * slope - sb[at : at + step, :]
+            e1[at : at + step, cols] = score
+            here = peaked(score)
+            top = here if top is None else jnp.maximum(top, here)
+        return jnp.max(top, axis=0, keepdims=True)
+
+    tops = [first_scores(0)]
+    for j in range(groups):
+        if j + 1 < groups:
+            tops.append(first_scores(j + 1))
+        values = expo_block(slice(j * block, (j + 1) * block), tops[j], e1, None)
+        if j == 0:
+            pl.semaphore_wait(barrier, chips + groups - 1)
+        send_stats(0, j, values)
     ct[...] = c[...].astype(F32).T.astype(BF16)
 
     def combine(which, j):
@@ -259,25 +270,48 @@
 
     def to_all(which, own, everywhere):
         at = rows_from(vec)
-        for far in range(1, chips):
+        for far in sorted(range(1, chips), key=lambda far: abs(far - chips // 2)):
             start(
                 own, everywhere.at[at, :],
                 all_send.at[which], all_recv.at[which, chips - far],
                 {"vec": chip_at(far) * CORES + core},
             )
-        start(own, everywhere.at[at, :], both_send.at[which], both_recv.at[which], sibling)
+        start(own, everywhere.at[at, :], both_send.at[which], both_recv.at[which, 0], sibling)
         everywhere[at, :] = own[...]
 
-    def wait_all(which, everywhere):
-        for k in range(1, chips):
-            far = (k + 1) // 2 if k % 2 else chips - k // 2
-            at = rows_from(chip_at(far) * CORES + core)
-            wait(everywhere.at[at, :], all_recv.at[which, far])
-            start(
-                everywhere.at[at, :], everywhere.at[at, :],
-                both_send.at[which], both_recv.at[which], sibling,
-            )
-        wait(everywhere.at[0 : chips * share, :], both_recv.at[which])
+    turns = sorted(range(ring_y), key=lambda d: min(d, ring_y - d))
+
+    def sources(n):
+        row = lax.rem(y + turns[n], ring_y)
+        for d in range(PAIR):
+            there = row * PAIR + lax.rem(x_low + d, PAIR)
+            yield turns[n] or d, there, lax.rem(there - chip + chips, chips)
+
+    def arrive(which, everywhere, n):
+        for other_chip, there, far in sources(n):
+            if other_chip:
+                at = rows_from(there * CORES + core)
+                wait(everywhere.at[at, :], all_recv.at[which, far])
+                start(
+                    everywhere.at[at, :], everywhere.at[at, :],
+                    both_send.at[which], both_recv.at[which, far], sibling,
+                )
+
+    def gathered(which, everywhere, work):
+        def finish(n):
+            for _, there, far in sources(n):
+                at = rows_from(there * CORES + 1 - core)
+                wait(everywhere.at[at, :], both_recv.at[which, far])
+            if work is not None:
+                work(lax.rem(y + turns[n], ring_y))
+
+        arrive(which, everywhere, 0)
+        finish(0)
+        arrive(which, everywhere, 1)
+        for n in range(1, ring_y):
+            if n + 1 < ring_y:
+                arrive(which, everywhere, n + 1)
+            finish(n)
 
     def mass_chunk(r):
         base = r * rows_of
@@ -305,17 +339,28 @@
     den[...] = column[rows_from(lax.rem(vec, owners)), :] + 1e-6
     own_moved[...] = (summed_up(0) / wide(den[...], depth)).astype(BF16)
     to_all(0, own_moved, moved)
-    wait_all(0, moved)
-
-    squares(moved)
+
+    loads[2].wait()
+    top_acc[...] = jnp.full_like(top_acc, -jnp.inf)
+
+    def second_rows(r):
+        rows = rows_at(r)
+        own = moved[rows, :]
+        f = own.astype(F32)
+        square = jnp.sum(f * f, axis=1, keepdims=True) * offset
+        for j in range(groups):
+            cols = slice(j * block, (j + 1) * block)
+            score = dot_nt(own, w[cols, :]) * slope - square
+            e2[rows, cols] = score
+            top_acc[:, cols] = jnp.maximum(top_acc[:, cols], peaked(score))
+            ds[rows, cols] = dot_nt(own, g[cols, :])
+
+    gathered(0, moved, second_rows)
 
     def second_block(j, carry):
         cols = cols_of(j)
-        cross = dot_nt(moved[...], w[cols, :])
-        for at in range(0, cents, step):
-            e2[at : at + step, cols] = cross[at : at + step] * slope - sb[at : at + step, :]
-        ds[:, cols] = dot_nt(moved[...], g[cols, :])
-        send_stats(1, j, soften_block(cols, e2, ds))
+        top = jnp.max(top_acc[:, cols], axis=0, keepdims=True)
+        send_stats(1, j, expo_block(cols, top, e2, ds))
         return carry
 
     lax.fori_loop(0, groups, second_block, 0)
@@ -351,20 +396,39 @@
     by_chunks(1, cot_chunk)
 
     def part_block(j, carry):
-        cols = cols_of(j)
+        cols = pl.ds(pl.multiple_of(j * 2 * block, 2 * block), 2 * block)
         part[:, cols] = dot_nn(mt[...], eb[:, cols])
         return carry
 
-    lax.fori_loop(0, groups, part_block, 0)
+    lax.fori_loop(0, groups // 2, part_block, 0)
 
     own_mean[...] = (summed_up(1) / wide(den[...], depth)).astype(BF16)
     to_all(1, own_mean, mean)
-    wait_all(1, mean)
-
-    for at in range(0, cents, step):
-        here = slice(at, at + step)
-        total = jnp.sum(mean[here, :].astype(F32) * moved[here, :].astype(F32), axis=1, keepdims=True)
-        sb[here, :] = jnp.broadcast_to(total, (step, block))
+
+    top_acc[...] = jnp.zeros_like(top_acc)
+
+    def third_rows(r):
+        rows = rows_at(r)
+        own = mean[rows, :]
+        shift = jnp.sum(own.astype(F32) * moved[rows, :].astype(F32), axis=1, keepdims=True)
+        for j in range(groups):
+            cols = slice(j * block, (j + 1) * block)
+            dfirst = dot_nt(own, w[cols, :]) - shift
+            ds[rows, cols] = dfirst
+            top_acc[:, cols] += folded(e1[rows, cols] * dfirst)
+
+    gathered(1, mean, third_rows)
+    for j in range(groups):
+        cols = slice(j * block, (j + 1) * block)
+        send_stats(2, j, (jnp.sum(top_acc[:, cols], axis=0, keepdims=True) * row1[j, 0:1, :],))
+    mt[...] = mean[...].astype(F32).T.astype(BF16)
+
+    def mean_block(j, carry):
+        cols = pl.ds(pl.multiple_of(j * 2 * block, 2 * block), 2 * block)
+        part[:, cols] += dot_nn(mt[...], r1b[:, cols])
+        return carry
+
+    lax.fori_loop(0, groups // 2, mean_block, 0)
 
     in_half = groups // 2
 
@@ -373,21 +437,6 @@
         far_x = lax.rem(t, PAIR)
         two_z = lax.rem(z // 2 + 1 + t // PAIR, ring_z // 2)
         return h, h * in_half + far_x * (ring_z // 2) + two_z, far_x, two_z * 2
-
-    def third_block(u, carry):
-        j = block_at(u)[1]
-        cols = cols_of(j)
-        cross = dot_nt(mean[...], w[cols, :])
-        dots = 0.0
-        for at in range(0, cents, step):
-            dfirst = cross[at : at + step] - sb[at : at + step, :]
-            ds[at : at + step, cols] = dfirst
-            dots = dots + folded(e1[at : at + step, cols] * dfirst)
-        send_stats(2, j, (jnp.sum(dots, axis=0, keepdims=True) * row1[j, 0:1, :],))
-        return carry
-
-    lax.fori_loop(0, groups, third_block, 0)
-    mt[...] = mean[...].astype(F32).T.astype(BF16)
 
     def grad_block(u, carry):
         h, j, to_x, first_z = block_at(u)
@@ -411,7 +460,7 @@
             def _():
                 esum[at : at + step, :] += total
 
-        grad = part[:, cols] + dot_nn(mt[...], r1b[:, cols]) + dot_nn(ct[...], eb[:, cols])
+        grad = part[:, cols] + dot_nn(ct[...], eb[:, cols])
         grad = grad.astype(BF16)
         for q in range(2):
             to_z = first_z + q
@@ -472,7 +521,7 @@
     own_start[...] = summed_up(2).astype(BF16)
     to_all(2, own_start, start_all)
     over_x(1)
-    wait_all(2, start_all)
+    gathered(2, start_all, None)
     result = pltpu.make_async_copy(start_all, gc, local.at[2])
     result.start()
     wait(gw.at[0 : (groups - 1) * 2 * piece, :], out_recv)
@@ -508,6 +557,10 @@
     vmem = pltpu.VMEM
     dma = pltpu.SemaphoreType.DMA
     scratch = [
+        vmem((vectors, depth), BF16),
+        vmem((cents, depth), BF16),
+        vmem((vectors, depth), BF16),
+        vmem((8, vectors), F32),
         vmem((cents, vectors), F32),
         vmem((cents, vectors), F32),
         vmem((cents, vectors), F32),
@@ -556,14 +609,14 @@
         dma((3,)),
         dma((3, chips)),
         dma((3,)),
-        dma((3,)),
+        dma((3, chips)),
         dma,
         dma((2,)),
         dma,
         dma((2,)),
         dma,
         dma,
-        dma((3,)),
+        dma((6,)),
     ]
     grad_rows, start_cot = pl.pallas_call(
         functools.partial(kernel, peers, groups),
@@ -571,7 +624,7 @@
             jax.ShapeDtypeStruct((vectors, depth), BF16),
             jax.ShapeDtypeStruct((cents, depth), BF16),
         ),
-        in_specs=[pl.BlockSpec(memory_space=pltpu.VMEM)] * 3,
+        in_specs=[pl.BlockSpec(memory_space=pl.ANY)] * 3,
         out_specs=[pl.BlockSpec(memory_space=pl.ANY)] * 2,
         scratch_shapes=scratch,
         compiler_params=pltpu.CompilerParams(

time: 101 us -> 98 us (0.970)
  Pallas kernels: 97.1 us -> 94 us
    pallas_call x1, Pallas kernels: 97.1 us -> 94 us  [body(): pl.pallas_call(functools.partial(kernel, peers, groups), out_shape=(jax.S...]
where the time goes in v3:
time: 98 us; the launch traced here: 97.8 us
  Pallas kernels  94 us (96%)
  other arithmetic  2.17 us (2%)
    pallas_call x1, Pallas kernels, body(): pl.pallas_call(functools.partial(kernel, peers, groups), out_shape=(jax.S...  94 us
    convert_element_type x1, other arithmetic, body(): return (grad_rows, start_cot.astype(F32))  2.17 us

profile of v3, /device:TPU:0, one launch (start us, length us, event | category | flops | bytes accessed | tf_op | source)
XLA Modules:
  0.0 97.8 jit_solution(9773977483428886275)
XLA Ops:
  0.6 94.0 %soft_assignments.1 = (bf16[2048,256]{1,0:T(8,128)(2,1)}, bf16[1024,256]{1,0:T(8,128)(2,1)}) custom-call(bf16[2048,256]{1,0:T(8,128)(2,1)} %w_hbm.1, bf16[1024,256]{1,0:T(8,128)(2,1)} %c_hbm.1, bf16[2048,256]{1,0:T(8,128)(2,1)} %g_hbm.1), custom_call_target="tpu_custom_call" | custom-call | tf_op jit(solution)/shard_map/soft_assignments/pallas_call | solution.py:621
  94.7 0.0 copy-start
  94.7 2.2 %convert_element_type.3 = f32[1024,256]{1,0:T(8,128)} convert(bf16[1024,256]{1,0:T(8,128)(2,1)} %get-tuple-element.5) | non-fusion elementwise | flops 262144 | bytes 1572864 | tf_op jit(solution)/shard_map/convert_element_type | solution.py:635
  96.9 0.0 copy-done
  96.9 1.0 copy.6
Async XLA Ops:
  94.7 2.2 %copy-start = (bf16[2048,256]{1,0:T(8,128)(2,1)S(1)}, bf16[2048,256]{1,0:T(8,128)(2,1)}, u32[]{:S(2)}) copy-start(bf16[2048,256]{1,0:T(8,128)(2,1)} %get-tuple-element.8) | copy-start | bytes 3145732

commit v4 on v3

--- a/solution.py
+++ b/solution.py
@@ -48,7 +48,7 @@
     w, c, g, top_acc,
     e1, e2, ds, r1b, r2b, eb, sb, ct, mt, moved, mean, part, esum, column, den,
     stat_out, stat_in, row1, row2, cnt_out, cnt_near, cnt_both, cnt_in, near_out, near_in, sum_out, sum_in,
-    own_moved, own_mean, own_start, start_all, grad_out, grad_in, pair_keep, pair_out, pair_in, own_grad,
+    own_moved, own_mean, own_start, start_all, grad_out, grad_in, pair_out, pair_in, own_grad,
     stat_send, stat_recv, near_send, near_recv, cnt_send, cnt_recv, sum_send, sum_recv, all_send, all_recv,
     both_send, both_recv, grad_send, grad_recv, pair_send, pair_recv, out_send, out_recv, local,
 ):
@@ -129,12 +129,14 @@
             return top, total
         return top, total, jnp.sum(dots, axis=0, keepdims=True)
 
-    def send_stats(which, j, values):
-        lanes = slice(0, len(values) * block)
+    def keep_stats(which, j, values):
         for line, value in enumerate(values):
             inner = slice(line * block, (line + 1) * block)
             stat_out[which, j, :, inner] = value
             stat_in[which, j, 0, :, inner] = value
+
+    def send_stats(which, j):
+        lanes = slice(0, STATS[which] * block)
         for far in range(1, groups):
             start(
                 stat_out.at[which, j, :, lanes],
@@ -173,10 +175,10 @@
     for j in range(groups):
         if j + 1 < groups:
             tops.append(first_scores(j + 1))
-        values = expo_block(slice(j * block, (j + 1) * block), tops[j], e1, None)
-        if j == 0:
-            pl.semaphore_wait(barrier, chips + groups - 1)
-        send_stats(0, j, values)
+        keep_stats(0, j, expo_block(slice(j * block, (j + 1) * block), tops[j], e1, None))
+    pl.semaphore_wait(barrier, chips + groups - 1)
+    for j in range(groups):
+        send_stats(0, j)
     ct[...] = c[...].astype(F32).T.astype(BF16)
 
     def combine(which, j):
@@ -192,12 +194,10 @@
         mine = jnp.exp2(stat(which, j, 0, 0) - peak)
         return mine / total, dots / total
 
-    def first_factor(j, carry):
+    for j in range(groups):
         wait_stats(0, j)
+    for j in range(groups):
         row1[j, 0:1, :] = combine(0, j)[0]
-        return carry
-
-    lax.fori_loop(0, groups, first_factor, 0)
 
     def to_sibling(which, r, value):
         for q in range(owners):
@@ -268,17 +268,6 @@
             total = total + sum_in[which, q].astype(F32)
         return total
 
-    def to_all(which, own, everywhere):
-        at = rows_from(vec)
-        for far in sorted(range(1, chips), key=lambda far: abs(far - chips // 2)):
-            start(
-                own, everywhere.at[at, :],
-                all_send.at[which], all_recv.at[which, chips - far],
-                {"vec": chip_at(far) * CORES + core},
-            )
-        start(own, everywhere.at[at, :], both_send.at[which], both_recv.at[which, 0], sibling)
-        everywhere[at, :] = own[...]
-
     turns = sorted(range(ring_y), key=lambda d: min(d, ring_y - d))
 
     def sources(n):
@@ -286,6 +275,20 @@
         for d in range(PAIR):
             there = row * PAIR + lax.rem(x_low + d, PAIR)
             yield turns[n] or d, there, lax.rem(there - chip + chips, chips)
+
+    def to_all(which, own, everywhere):
+        at = rows_from(vec)
+        for n in range(ring_y):
+            for other_chip, there, far in sources(n):
+                if other_chip:
+                    start(
+                        own, everywhere.at[at, :],
+                        all_send.at[which], all_recv.at[which, lax.rem(chips - far, chips)],
+                        {"vec": there * CORES + core},
+                    )
+                else:
+                    start(own, everywhere.at[at, :], both_send.at[which], both_recv.at[which, 0], sibling)
+        everywhere[at, :] = own[...]
 
     def arrive(which, everywhere, n):
         for other_chip, there, far in sources(n):
@@ -315,15 +318,17 @@
 
     def mass_chunk(r):
         base = r * rows_of
-        for at in range(0, rows_of, step):
-            here = pl.ds(pl.multiple_of(base + at, step), step)
-            count = 0.0
-            for j in range(groups):
-                cols = slice(j * block, (j + 1) * block)
+        ats = range(0, rows_of, step)
+        counts = [0.0] * len(ats)
+        for j in range(groups):
+            cols = slice(j * block, (j + 1) * block)
+            for n, at in enumerate(ats):
+                here = pl.ds(pl.multiple_of(base + at, step), step)
                 resp = e1[here, cols] * row1[j, 0:1, :]
                 r1b[here, cols] = resp.astype(BF16)
-                count = count + lane_folded(resp)
-            count = jnp.sum(count, axis=1, keepdims=True)
+                counts[n] = counts[n] + lane_folded(resp)
+        for n, at in enumerate(ats):
+            count = jnp.sum(counts[n], axis=1, keepdims=True)
             column[at : at + step, :] = jnp.broadcast_to(count, (step, LANES))
         cnt_out[r] = column[...].T[0:1, :]
         to_sibling(0, r, dot_nn(r1b[rows_at(r), :], w[...]))
@@ -360,35 +365,36 @@
     def second_block(j, carry):
         cols = cols_of(j)
         top = jnp.max(top_acc[:, cols], axis=0, keepdims=True)
-        send_stats(1, j, expo_block(cols, top, e2, ds))
+        keep_stats(1, j, expo_block(cols, top, e2, ds))
+        send_stats(1, j)
         return carry
 
     lax.fori_loop(0, groups, second_block, 0)
     mt[...] = moved[...].astype(F32).T.astype(BF16)
 
-    def second_factor(j, carry):
+    for j in range(groups):
         wait_stats(1, j)
+    for j in range(groups):
         factor, dots = combine(1, j)
         row2[j, 0:1, :] = factor
         row2[j, 1:2, :] = dots
-        return carry
-
-    lax.fori_loop(0, groups, second_factor, 0)
 
     def cot_chunk(r):
         base = r * rows_of
         rows = rows_at(r)
-        for at in range(0, rows_of, step):
-            here = pl.ds(pl.multiple_of(base + at, step), step)
-            total = 0.0
-            for j in range(groups):
-                cols = slice(j * block, (j + 1) * block)
+        ats = range(0, rows_of, step)
+        totals = [0.0] * len(ats)
+        for j in range(groups):
+            cols = slice(j * block, (j + 1) * block)
+            for n, at in enumerate(ats):
+                here = pl.ds(pl.multiple_of(base + at, step), step)
                 second = e2[here, cols] * row2[j, 0:1, :]
                 r2b[here, cols] = second.astype(BF16)
                 edge = second * (ds[here, cols] - row2[j, 1:2, :]) * scale
                 eb[here, cols] = edge.astype(BF16)
-                total = total + lane_folded(edge)
-            total = jnp.sum(total, axis=1, keepdims=True)
+                totals[n] = totals[n] + lane_folded(edge)
+        for n, at in enumerate(ats):
+            total = jnp.sum(totals[n], axis=1, keepdims=True)
             column[at : at + step, :] = jnp.broadcast_to(total, (step, LANES))
         cot = dot_nn(r2b[rows, :], g[...]) + dot_nn(eb[rows, :], w[...])
         to_sibling(1, r, cot - wide(column[...], depth) * moved[rows, :].astype(F32))
@@ -420,7 +426,8 @@
     gathered(1, mean, third_rows)
     for j in range(groups):
         cols = slice(j * block, (j + 1) * block)
-        send_stats(2, j, (jnp.sum(top_acc[:, cols], axis=0, keepdims=True) * row1[j, 0:1, :],))
+        keep_stats(2, j, (jnp.sum(top_acc[:, cols], axis=0, keepdims=True) * row1[j, 0:1, :],))
+        send_stats(2, j)
     mt[...] = mean[...].astype(F32).T.astype(BF16)
 
     def mean_block(j, carry):
@@ -486,27 +493,34 @@
 
     other = {"cent": (1 - x_high) * ring_z + z}
 
-    def over_z(h):
-        wait(grad_in.at[h, 1:ring_z], grad_recv.at[h])
-
-        def total(to_x):
-            value = grad_in[h, 0, to_x].astype(F32)
+    part_d = depth // 2
+
+    def over_z(h, n):
+        if n == 0:
+            wait(grad_in.at[h, 1:ring_z], grad_recv.at[h])
+        for to_x in range(PAIR):
+            inner = slice(n * part_d, (n + 1) * part_d)
+            total = grad_in[h, 0, to_x, inner, :].astype(F32)
             for q in range(1, ring_z):
-                value = value + grad_in[h, q, to_x].astype(F32)
-            return value
-
-        pair_out[h] = total(1 - x_high).astype(BF16)
-        start(pair_out.at[h], pair_in.at[h], pair_send, pair_recv.at[h], other)
-        pair_keep[h] = total(x_high)
-
-    def over_x(h):
-        wait(pair_in.at[h], pair_recv.at[h])
-        total = pair_keep[h] + pair_in[h].astype(F32)
-        own_grad[h] = total.T.astype(BF16)
-        rows = pl.ds(pl.multiple_of(h * half + cent * piece, piece), piece)
-        for far in range(1, groups):
-            start(own_grad.at[h], gw.at[rows, :], out_send, out_recv, cent_at(far))
-        pltpu.make_async_copy(own_grad.at[h], gw.at[rows, :], local.at[h]).start()
+                total = total + grad_in[h, q, to_x, inner, :].astype(F32)
+            pair_out[h, n, to_x] = total.astype(BF16)
+        start(pair_out.at[h, n], pair_in.at[h, n], pair_send, pair_recv.at[h, n], other)
+
+    def grad_place(h, n, to_x):
+        rows = h * half + (to_x * ring_z + z) * piece
+        return gw.at[pl.ds(pl.multiple_of(rows, piece), piece), n * part_d : (n + 1) * part_d]
+
+    def over_x(h, n):
+        wait(pair_in.at[h, n], pair_recv.at[h, n])
+        for to_x in range(PAIR):
+            total = pair_out[h, n, to_x].astype(F32) + pair_in[h, n, to_x].astype(F32)
+            own_grad[h, n, to_x] = total.T.astype(BF16)
+        for to_x in range(PAIR):
+            place = grad_place(h, n, to_x)
+            for far in range(1, ring_z):
+                there = {"cent": x_high * ring_z + lax.rem(z + far, ring_z)}
+                start(own_grad.at[h, n, to_x], place, out_send, out_recv, there)
+            pltpu.make_async_copy(own_grad.at[h, n, to_x], place, local.at[h]).start()
 
     def start_chunk(r):
         rows = rows_at(r)
@@ -514,19 +528,23 @@
         value = dot_nn(eb[rows, :], w[...]) - total * c[rows, :].astype(F32)
         to_sibling(2, r, value)
 
-    over_z(0)
+    over_z(0, 0)
+    over_z(0, 1)
     by_chunks(2, start_chunk)
-    over_x(0)
-    over_z(1)
+    over_x(0, 0)
+    over_x(0, 1)
+    over_z(1, 0)
+    over_z(1, 1)
     own_start[...] = summed_up(2).astype(BF16)
     to_all(2, own_start, start_all)
-    over_x(1)
+    over_x(1, 0)
+    over_x(1, 1)
     gathered(2, start_all, None)
     result = pltpu.make_async_copy(start_all, gc, local.at[2])
     result.start()
-    wait(gw.at[0 : (groups - 1) * 2 * piece, :], out_recv)
+    wait(gw.at[0 : (ring_z - 1) * 2 * PAIR * piece, :], out_recv)
     for h in range(2):
-        pltpu.make_async_copy(own_grad.at[h], gw.at[0:piece, :], local.at[h]).wait()
+        wait(gw.at[0 : PAIR * piece, :], local.at[h])
     result.wait()
 
     for which in range(3):
@@ -540,7 +558,7 @@
     wait(cnt_in.at[1:chips], cnt_send.at[1])
     wait(grad_in.at[:, 1:ring_z], grad_send)
     wait(pair_in, pair_send)
-    wait(gw.at[0 : (groups - 1) * 2 * piece, :], out_send)
+    wait(gw.at[0 : (ring_z - 1) * 2 * PAIR * piece, :], out_send)
 
 
 def body(peers, groups, weights, centroids, cotangent):
@@ -594,10 +612,9 @@
         vmem((cents, depth), BF16),
         vmem((2, PAIR, ring_z, depth, piece), BF16),
         vmem((2, ring_z, PAIR, depth, piece), BF16),
-        vmem((2, depth, piece), F32),
-        vmem((2, depth, piece), BF16),
-        vmem((2, depth, piece), BF16),
-        vmem((2, piece, depth), BF16),
+        vmem((2, 2, PAIR, depth // 2, piece), BF16),
+        vmem((2, 2, PAIR, depth // 2, piece), BF16),
+        vmem((2, 2, PAIR, piece, depth // 2), BF16),
         dma((3,)),
         dma((3, groups)),
         dma((3,)),
@@ -613,7 +630,7 @@
         dma,
         dma((2,)),
         dma,
-        dma((2,)),
+        dma((2, 2)),
         dma,
         dma,
         dma((6,)),

time: 98 us -> 91.5 us (0.934)
  Pallas kernels: 94 us -> 87.5 us
    pallas_call x1, Pallas kernels: 94 us -> 87.5 us  [body(): pl.pallas_call(functools.partial(kernel, peers, groups), out_shape=(jax.S...]
where the time goes in v4:
time: 91.5 us; the launch traced here: 91.3 us
  Pallas kernels  87.5 us (96%)
  other arithmetic  2.17 us (2%)
  local copies, waits for them, and re-layouts  0.97 us (1%)
    pallas_call x1, Pallas kernels, body(): pl.pallas_call(functools.partial(kernel, peers, groups), out_shape=(jax.S...  87.5 us
    convert_element_type x1, other arithmetic, body(): return (grad_rows, start_cot.astype(F32))  2.17 us

profile of v4, /device:TPU:0, one launch (start us, length us, event | category | flops | bytes accessed | tf_op | source)
XLA Modules:
  0.0 91.3 jit_solution(7616519871794510179)
XLA Ops:
  0.6 87.5 %soft_assignments.1 = (bf16[2048,256]{1,0:T(8,128)(2,1)}, bf16[1024,256]{1,0:T(8,128)(2,1)}) custom-call(bf16[2048,256]{1,0:T(8,128)(2,1)} %w_hbm.1, bf16[1024,256]{1,0:T(8,128)(2,1)} %c_hbm.1, bf16[2048,256]{1,0:T(8,128)(2,1)} %g_hbm.1), custom_call_target="tpu_custom_call" | custom-call | tf_op jit(solution)/shard_map/soft_assignments/pallas_call | solution.py:638
  88.1 0.0 copy-start
  88.1 2.2 %convert_element_type.3 = f32[1024,256]{1,0:T(8,128)} convert(bf16[1024,256]{1,0:T(8,128)(2,1)} %get-tuple-element.5) | non-fusion elementwise | flops 262144 | bytes 1572864 | tf_op jit(solution)/shard_map/convert_element_type | solution.py:652
  90.3 0.0 copy-done
  90.3 1.0 %copy.6 = bf16[2048,256]{1,0:T(8,128)(2,1)} copy(bf16[2048,256]{1,0:T(8,128)(2,1)S(1)} %copy-done) | data formatting | bytes 2097152
Async XLA Ops:
  88.1 2.2 %copy-start = (bf16[2048,256]{1,0:T(8,128)(2,1)S(1)}, bf16[2048,256]{1,0:T(8,128)(2,1)}, u32[]{:S(2)}) copy-start(bf16[2048,256]{1,0:T(8,128)(2,1)} %get-tuple-element.8) | copy-start | bytes 3145732

commit v5 on v4

--- a/solution.py
+++ b/solution.py
@@ -83,6 +83,9 @@
     def wait(ref, sem):
         pltpu.make_async_copy(ref, ref, sem).wait()
 
+    def apart(work):
+        pl.when(vec >= 0)(work)
+
     def cent_at(far):
         return {"cent": lax.rem(cent + far, groups)}
 
@@ -98,13 +101,19 @@
     def rows_at(r):
         return pl.ds(pl.multiple_of(r * rows_of, rows_of), rows_of)
 
-    def rows_from(owner):
-        return pl.ds(pl.multiple_of(owner * share, share), share)
+    def chunk(t):
+        return slice(t * rows_of, (t + 1) * rows_of)
+
+    def place(t, low, of_core):
+        at = t * rows_of + (low * CORES + of_core) * share
+        return pl.ds(pl.multiple_of(at, share), share)
 
     loads = [
         pltpu.make_async_copy(src, dst, local.at[3 + n])
-        for n, (src, dst) in enumerate(((c_hbm, c), (w_hbm, w), (g_hbm, g)))
+        for n, (src, dst) in enumerate(((w_hbm, w), (g_hbm, g)))
     ]
+    for t in range(ring_y):
+        pltpu.make_async_copy(c_hbm.at[rows_at(chunk_of(t)), :], c.at[chunk(t), :], local.at[5]).start()
     for load in loads:
         load.start()
 
@@ -153,12 +162,12 @@
     def stat(which, j, q, line):
         return stat_in[which, j, q, :, line * block : (line + 1) * block]
 
-    loads[0].wait()
+    pltpu.make_async_copy(c, c, local.at[5]).wait()
     for at in range(0, cents, step):
         f = c[at : at + step, :].astype(F32)
         total = jnp.sum(f * f, axis=1, keepdims=True) * offset
         sb[at : at + step, :] = jnp.broadcast_to(total, (step, block))
-    loads[1].wait()
+    loads[0].wait()
 
     def first_scores(j):
         cols = slice(j * block, (j + 1) * block)
@@ -199,67 +208,56 @@
     for j in range(groups):
         row1[j, 0:1, :] = combine(0, j)[0]
 
-    def to_sibling(which, r, value):
-        for q in range(owners):
-            near_out[which, r, q] = value[q * share : (q + 1) * share]
+    def to_sibling(which, t):
         for q in range(PAIR):
             theirs = q * CORES + 1 - core
             start(
-                near_out.at[which, r, theirs],
-                near_in.at[which, r, q],
+                near_out.at[which, t, theirs],
+                near_in.at[which, t, q],
                 near_send.at[which],
-                near_recv.at[which, r],
+                near_recv.at[which, t],
                 sibling,
             )
-
-    def to_owners(which, r):
-        wait(near_in.at[which, r], near_recv.at[which, r])
         if which == 0:
-            wait(cnt_near.at[r], cnt_recv.at[r])
-            cnt_both[r] = cnt_out[r] + cnt_near[r]
-
-        def one(q, carry):
-            total = near_out[which, r, q * CORES + core] + near_in[which, r, q]
-            there = r * PAIR + q
-            far = lax.rem(there - chip + chips, chips)
-            slot = lax.rem(chips - far, chips)
-            sum_out[which, there] = total.astype(BF16)
-
-            @pl.when(far != 0)
-            def _():
-                device = {"vec": there * CORES + core}
-                start(
-                    sum_out.at[which, there], sum_in.at[which, slot],
-                    sum_send.at[which], sum_recv.at[which], device,
-                )
-                if which == 0:
-                    start(
-                        cnt_both.at[r], cnt_in.at[slot],
-                        cnt_send.at[1], cnt_recv.at[ring_y], device,
-                    )
-
-            @pl.when(far == 0)
-            def _():
+            start(cnt_out.at[t], cnt_near.at[t], cnt_send.at[0], cnt_recv.at[t], sibling)
+
+    def to_owners(which, t):
+        wait(near_in.at[which, t], near_recv.at[which, t])
+        if which == 0:
+            wait(cnt_near.at[t], cnt_recv.at[t])
+            cnt_both[t] = cnt_out[t] + cnt_near[t]
+        for d in range(PAIR):
+            low = lax.rem(x_low + d, PAIR)
+            total = near_out[which, t, low * CORES + core] + near_in[which, t, low]
+            if t == ring_y - 1 and d == 0:
                 sum_in[which, 0] = total.astype(BF16)
                 if which == 0:
-                    cnt_in[0] = cnt_both[r]
-
-            return carry
-
-        lax.fori_loop(0, PAIR, one, 0)
-
-    def by_chunks(which, chunk):
-        def one(t, carry):
-            chunk(chunk_of(t))
-
-            @pl.when(t > 0)
+                    cnt_in[0] = cnt_both[t]
+                continue
+            n = t * PAIR + d
+            sum_out[which, n] = total.astype(BF16)
+            there = chunk_of(t) * PAIR + low
+            slot = lax.rem(chip - there + chips, chips)
+            device = {"vec": there * CORES + core}
+            start(sum_out.at[which, n], sum_in.at[which, slot], sum_send.at[which], sum_recv.at[which], device)
+            if which == 0:
+                start(cnt_both.at[t], cnt_in.at[slot], cnt_send.at[1], cnt_recv.at[ring_y], device)
+
+    def by_chunks(which, prepare, product):
+        for t in range(ring_y):
+
+            @apart
             def _():
-                to_owners(which, chunk_of(t - 1))
-
-            return carry
-
-        lax.fori_loop(0, ring_y, one, 0)
-        to_owners(which, chunk_of(ring_y - 1))
+                prepare(t)
+                value = product(t)
+                for q in range(owners):
+                    near_out[which, t, q] = value[q * share : (q + 1) * share]
+
+            to_sibling(which, t)
+            if t > 1:
+                to_owners(which, t - 2)
+        for t in range(ring_y - 2, ring_y):
+            to_owners(which, t)
 
     def summed_up(which):
         wait(sum_in.at[which, 1:chips], sum_recv.at[which])
@@ -273,13 +271,17 @@
     def sources(n):
         row = lax.rem(y + turns[n], ring_y)
         for d in range(PAIR):
-            there = row * PAIR + lax.rem(x_low + d, PAIR)
-            yield turns[n] or d, there, lax.rem(there - chip + chips, chips)
+            low = lax.rem(x_low + d, PAIR)
+            there = row * PAIR + low
+            yield turns[n] or d, there, low, lax.rem(there - chip + chips, chips)
+
+    def chunk_in(n):
+        return (turns[n] - 1) % ring_y
 
     def to_all(which, own, everywhere):
-        at = rows_from(vec)
         for n in range(ring_y):
-            for other_chip, there, far in sources(n):
+            at = place((-turns[n] - 1) % ring_y, x_low, core)
+            for other_chip, there, _, far in sources(n):
                 if other_chip:
                     start(
                         own, everywhere.at[at, :],
@@ -288,12 +290,12 @@
                     )
                 else:
                     start(own, everywhere.at[at, :], both_send.at[which], both_recv.at[which, 0], sibling)
-        everywhere[at, :] = own[...]
+        everywhere[place(ring_y - 1, x_low, core), :] = own[...]
 
     def arrive(which, everywhere, n):
-        for other_chip, there, far in sources(n):
+        for other_chip, _, low, far in sources(n):
             if other_chip:
-                at = rows_from(there * CORES + core)
+                at = place(chunk_in(n), low, core)
                 wait(everywhere.at[at, :], all_recv.at[which, far])
                 start(
                     everywhere.at[at, :], everywhere.at[at, :],
@@ -302,11 +304,11 @@
 
     def gathered(which, everywhere, work):
         def finish(n):
-            for _, there, far in sources(n):
-                at = rows_from(there * CORES + 1 - core)
+            for _, _, low, far in sources(n):
+                at = place(chunk_in(n), low, 1 - core)
                 wait(everywhere.at[at, :], both_recv.at[which, far])
             if work is not None:
-                work(lax.rem(y + turns[n], ring_y))
+                apart(lambda: work(chunk_in(n)))
 
         arrive(which, everywhere, 0)
         finish(0)
@@ -316,40 +318,39 @@
                 arrive(which, everywhere, n + 1)
             finish(n)
 
-    def mass_chunk(r):
-        base = r * rows_of
-        ats = range(0, rows_of, step)
-        counts = [0.0] * len(ats)
+    def lane_sums(at, totals):
+        for n, total in enumerate(totals):
+            here = slice(at + n * step, at + (n + 1) * step)
+            column[here, :] = jnp.broadcast_to(jnp.sum(total, axis=1, keepdims=True), (step, LANES))
+
+    def mass_prepare(t):
+        counts = [0.0] * (rows_of // step)
         for j in range(groups):
             cols = slice(j * block, (j + 1) * block)
-            for n, at in enumerate(ats):
-                here = pl.ds(pl.multiple_of(base + at, step), step)
+            for n in range(len(counts)):
+                here = slice(t * rows_of + n * step, t * rows_of + (n + 1) * step)
                 resp = e1[here, cols] * row1[j, 0:1, :]
                 r1b[here, cols] = resp.astype(BF16)
                 counts[n] = counts[n] + lane_folded(resp)
-        for n, at in enumerate(ats):
-            count = jnp.sum(counts[n], axis=1, keepdims=True)
-            column[at : at + step, :] = jnp.broadcast_to(count, (step, LANES))
-        cnt_out[r] = column[...].T[0:1, :]
-        to_sibling(0, r, dot_nn(r1b[rows_at(r), :], w[...]))
-        start(cnt_out.at[r], cnt_near.at[r], cnt_send.at[0], cnt_recv.at[r], sibling)
-
-    by_chunks(0, mass_chunk)
+        lane_sums(t * rows_of, counts)
+        cnt_out[t] = column[chunk(t), :].T[0:1, :]
+
+    by_chunks(0, mass_prepare, lambda t: dot_nn(r1b[chunk(t), :], w[...]))
 
     wait(cnt_in.at[1:chips], cnt_recv.at[ring_y])
     count = cnt_in[0]
     for q in range(1, chips):
         count = count + cnt_in[q]
-    column[...] = jnp.broadcast_to(count, (LANES, rows_of)).T
-    den[...] = column[rows_from(lax.rem(vec, owners)), :] + 1e-6
+    column[chunk(0), :] = jnp.broadcast_to(count, (LANES, rows_of)).T
+    den[...] = column[place(0, x_low, core), :] + 1e-6
     own_moved[...] = (summed_up(0) / wide(den[...], depth)).astype(BF16)
     to_all(0, own_moved, moved)
 
-    loads[2].wait()
+    loads[1].wait()
     top_acc[...] = jnp.full_like(top_acc, -jnp.inf)
 
-    def second_rows(r):
-        rows = rows_at(r)
+    def second_rows(t):
+        rows = chunk(t)
         own = moved[rows, :]
         f = own.astype(F32)
         square = jnp.sum(f * f, axis=1, keepdims=True) * offset
@@ -379,27 +380,25 @@
         row2[j, 0:1, :] = factor
         row2[j, 1:2, :] = dots
 
-    def cot_chunk(r):
-        base = r * rows_of
-        rows = rows_at(r)
-        ats = range(0, rows_of, step)
-        totals = [0.0] * len(ats)
+    def cot_prepare(t):
+        totals = [0.0] * (rows_of // step)
         for j in range(groups):
             cols = slice(j * block, (j + 1) * block)
-            for n, at in enumerate(ats):
-                here = pl.ds(pl.multiple_of(base + at, step), step)
+            for n in range(len(totals)):
+                here = slice(t * rows_of + n * step, t * rows_of + (n + 1) * step)
                 second = e2[here, cols] * row2[j, 0:1, :]
                 r2b[here, cols] = second.astype(BF16)
                 edge = second * (ds[here, cols] - row2[j, 1:2, :]) * scale
                 eb[here, cols] = edge.astype(BF16)
                 totals[n] = totals[n] + lane_folded(edge)
-        for n, at in enumerate(ats):
-            total = jnp.sum(totals[n], axis=1, keepdims=True)
-            column[at : at + step, :] = jnp.broadcast_to(total, (step, LANES))
+        lane_sums(t * rows_of, totals)
+
+    def cot_product(t):
+        rows = chunk(t)
         cot = dot_nn(r2b[rows, :], g[...]) + dot_nn(eb[rows, :], w[...])
-        to_sibling(1, r, cot - wide(column[...], depth) * moved[rows, :].astype(F32))
-
-    by_chunks(1, cot_chunk)
+        return cot - wide(column[rows, :], depth) * moved[rows, :].astype(F32)
+
+    by_chunks(1, cot_prepare, cot_product)
 
     def part_block(j, carry):
         cols = pl.ds(pl.multiple_of(j * 2 * block, 2 * block), 2 * block)
@@ -413,8 +412,8 @@
 
     top_acc[...] = jnp.zeros_like(top_acc)
 
-    def third_rows(r):
-        rows = rows_at(r)
+    def third_rows(t):
+        rows = chunk(t)
         own = mean[rows, :]
         shift = jnp.sum(own.astype(F32) * moved[rows, :].astype(F32), axis=1, keepdims=True)
         for j in range(groups):
@@ -522,15 +521,14 @@
                 start(own_grad.at[h, n, to_x], place, out_send, out_recv, there)
             pltpu.make_async_copy(own_grad.at[h, n, to_x], place, local.at[h]).start()
 
-    def start_chunk(r):
-        rows = rows_at(r)
+    def start_product(t):
+        rows = chunk(t)
         total = jnp.sum(esum[rows, :], axis=1, keepdims=True)
-        value = dot_nn(eb[rows, :], w[...]) - total * c[rows, :].astype(F32)
-        to_sibling(2, r, value)
+        return dot_nn(eb[rows, :], w[...]) - total * c[rows, :].astype(F32)
 
     over_z(0, 0)
     over_z(0, 1)
-    by_chunks(2, start_chunk)
+    by_chunks(2, lambda t: None, start_product)
     over_x(0, 0)
     over_x(0, 1)
     over_z(1, 0)
@@ -540,12 +538,13 @@
     over_x(1, 0)
     over_x(1, 1)
     gathered(2, start_all, None)
-    result = pltpu.make_async_copy(start_all, gc, local.at[2])
-    result.start()
+    for t in range(ring_y):
+        rows = rows_at(chunk_of(t))
+        pltpu.make_async_copy(start_all.at[chunk(t), :], gc.at[rows, :], local.at[2]).start()
     wait(gw.at[0 : (ring_z - 1) * 2 * PAIR * piece, :], out_recv)
     for h in range(2):
         wait(gw.at[0 : PAIR * piece, :], local.at[h])
-    result.wait()
+    wait(start_all, local.at[2])
 
     for which in range(3):
         lanes = slice(0, STATS[which] * block)
@@ -592,7 +591,7 @@
         vmem((cents, depth), BF16),
         vmem((depth, vectors), F32),
         vmem((cents, LANES), F32),
-        vmem((rows_of, LANES), F32),
+        vmem((cents, LANES), F32),
         vmem((share, LANES), F32),
         vmem((3, groups, 1, 3 * block), F32),
         vmem((3, groups, groups, 1, 3 * block), F32),

time: 91.5 us -> 90.2 us (0.986)
  Pallas kernels: 87.5 us -> 86.3 us
    pallas_call x1, Pallas kernels: 87.5 us -> 86.3 us  [body(): pl.pallas_call(functools.partial(kernel, peers, groups), out_shape=(jax.S...]
where the time goes in v5:
time: 90.2 us; the launch traced here: 90.1 us
  Pallas kernels  86.3 us (96%)
  other arithmetic  2.17 us (2%)
  local copies, waits for them, and re-layouts  0.97 us (1%)
    pallas_call x1, Pallas kernels, body(): pl.pallas_call(functools.partial(kernel, peers, groups), out_shape=(jax.S...  86.3 us
    convert_element_type x1, other arithmetic, body(): return (grad_rows, start_cot.astype(F32))  2.17 us

profile of v5, /device:TPU:0, one launch (start us, length us, event | category | flops | bytes accessed | tf_op | source)
XLA Modules:
  0.0 90.1 jit_solution(9087822935224944250)
XLA Ops:
  0.6 86.3 %soft_assignments.1 = (bf16[2048,256]{1,0:T(8,128)(2,1)}, bf16[1024,256]{1,0:T(8,128)(2,1)}) custom-call(bf16[2048,256]{1,0:T(8,128)(2,1)} %w_hbm.1, bf16[1024,256]{1,0:T(8,128)(2,1)} %c_hbm.1, bf16[2048,256]{1,0:T(8,128)(2,1)} %g_hbm.1), custom_call_target="tpu_custom_call" | custom-call | tf_op jit(solution)/shard_map/soft_assignments/pallas_call | solution.py:637
  86.9 0.0 copy-start
  86.9 2.2 %convert_element_type.3 = f32[1024,256]{1,0:T(8,128)} convert(bf16[1024,256]{1,0:T(8,128)(2,1)} %get-tuple-element.5) | non-fusion elementwise | flops 262144 | bytes 1572864 | tf_op jit(solution)/shard_map/convert_element_type | solution.py:651
  89.1 0.0 copy-done
  89.1 1.0 %copy.6 = bf16[2048,256]{1,0:T(8,128)(2,1)} copy(bf16[2048,256]{1,0:T(8,128)(2,1)S(1)} %copy-done) | data formatting | bytes 2097152
Async XLA Ops:
  86.9 2.2 %copy-start = (bf16[2048,256]{1,0:T(8,128)(2,1)S(1)}, bf16[2048,256]{1,0:T(8,128)(2,1)}, u32[]{:S(2)}) copy-start(bf16[2048,256]{1,0:T(8,128)(2,1)} %get-tuple-element.8) | copy-start | bytes 3145732
